TPU v7x, 32 devices: a whole 2x2x4 slice. The times are simulated.
32 devices in a mesh: ctx: 8 (over z, x), heads: 4 (over y, core).
Axes of the slice: x: 2, y: 2, z: 4, core: 2. Of those that a mesh axis runs over, the one named last changes fastest.
Arguments:
- activations: bfloat16 [2048, 8192], P('ctx', 'heads'), may hold values from -20 to 20
- w_query: bfloat16 [8192, 4096], P(None, 'heads'), may hold values from -0.0625 to 0.0625
- w_key: bfloat16 [8192, 1024], P(None, 'heads'), may hold values from -0.0625 to 0.0625
- w_value: bfloat16 [8192, 1024], P(None, 'heads'), may hold values from -0.0625 to 0.0625
- doc_lengths: int32 [8], replicated, may hold values from 1 to 1024, 2048 in all
- block_dest: int32 [32], replicated, may hold values from 0 to 7, as said below
- out_grad: bfloat16 [2048, 4096], P('ctx', 'heads'), may hold values from -6 to 6
Outputs:
- attention: bfloat16 [2048, 4096], P('ctx', 'heads')
- input_grad: bfloat16 [2048, 8192], P('ctx', 'heads')
Inputs may be any that keep to these rules, and one draw needn't show every extreme that they name: `block_dest`: loader block b lies on loader shard b // 4. Each loader shard sends its blocks to different context shards, and each context shard receives exactly 4 blocks, from different loader shards.
All inputs are finite; a program needn't handle non-finite values.
Results may differ from a plain program's by a relative error of at most 0.025.
The roundings to bfloat16 on the way count: a program that leaves them out, or rounds other values in their place, can miss the bound.
Values may be sent and summed in bfloat16 or wider, within the bound.
A program may use at most 128 MiB of HBM per device.

v0:
```python
import math
import jax
import jax.numpy as jnp
from jax import lax
from jax.sharding import PartitionSpec as P

HD = 128
QPK = 4
NEG = -1e30


def from_behind(value, axis, steps):
    count = lax.axis_size(axis)
    pairs = [(source, (source + steps) % count) for source in range(count)]
    return lax.ppermute(value, axis, pairs)


def layout(block_dest, block_rows):
    nblk = block_dest.shape[0]
    index = jnp.arange(nblk, dtype=jnp.int32)
    order_key = block_dest * nblk + index
    ranks = jnp.sum((order_key[None, :] < order_key[:, None]).astype(jnp.int32), axis=1)
    ctx_blocks = jnp.sum(jnp.where(ranks[None, :] == index[:, None], index[None, :], 0), axis=1)
    ctx_pos = (
        ctx_blocks[:, None] * block_rows + jnp.arange(block_rows, dtype=jnp.int32)[None, :]
    ).reshape(-1)
    return (ctx_blocks, ctx_pos)


def doc_ids(positions, doc_lengths):
    ends = jnp.cumsum(doc_lengths)
    return jnp.sum((ends[None, :] <= positions[:, None]).astype(jnp.int32), axis=1)


def spread(table, array, block_rows):
    width = array.shape[-1]
    grouped = array.reshape(table.shape[1], block_rows, width)
    moved = jnp.einsum("ab,brf->arf", table, grouped, preferred_element_type=jnp.float32)
    return moved.astype(jnp.bfloat16)


def transposed_dot(left, weight):
    return lax.dot_general(
        left, weight, (((1,), (1,)), ((), ())), preferred_element_type=jnp.float32
    )


def per_device(activations, w_query, w_key, w_value, doc_lengths, block_dest, out_grad):
    ctx_count = lax.axis_size("ctx")
    ctx_rank = lax.axis_index("ctx")
    tok_dev = activations.shape[0]
    block_rows = tok_dev * ctx_count // block_dest.shape[0]
    blocks_here = tok_dev // block_rows
    head_dim = HD
    groups = w_key.shape[1] // head_dim
    per_group = QPK
    scale = 1.0 / math.sqrt(head_dim)
    ctx_blocks, ctx_pos = layout(block_dest, block_rows)
    ctx_doc = doc_ids(ctx_pos, doc_lengths)
    my_pos = lax.dynamic_slice_in_dim(ctx_pos, ctx_rank * tok_dev, tok_dev, 0)
    my_doc = lax.dynamic_slice_in_dim(ctx_doc, ctx_rank * tok_dev, tok_dev, 0)
    piece = lax.all_gather(activations, "heads", axis=1, tiled=True)
    rows = piece.shape[1]
    proj_q = jnp.dot(piece, w_query, preferred_element_type=jnp.float32)
    proj_k = jnp.dot(piece, w_key, preferred_element_type=jnp.float32)
    proj_v = jnp.dot(piece, w_value, preferred_element_type=jnp.float32)
    loader_q = proj_q.astype(jnp.bfloat16)
    loader_k = proj_k.astype(jnp.bfloat16)
    loader_v = proj_v.astype(jnp.bfloat16)
    slots = jnp.arange(ctx_count, dtype=jnp.int32)
    my_dest = lax.dynamic_slice_in_dim(block_dest, ctx_rank * blocks_here, blocks_here, 0)
    send_map = (my_dest[None, :] == slots[:, None]).astype(jnp.bfloat16)
    mine = lax.dynamic_slice_in_dim(ctx_blocks, ctx_rank * blocks_here, blocks_here, 0)
    source = mine // blocks_here
    take_map = (source[:, None] == slots[None, :]).astype(jnp.bfloat16)
    recv_q, recv_k, recv_v = (
        lax.all_to_all(
            spread(send_map, loader_q, block_rows), "ctx", split_axis=0, concat_axis=0, tiled=True
        ),
        lax.all_to_all(
            spread(send_map, loader_k, block_rows), "ctx", split_axis=0, concat_axis=0, tiled=True
        ),
        lax.all_to_all(
            spread(send_map, loader_v, block_rows), "ctx", split_axis=0, concat_axis=0, tiled=True
        ),
    )
    ctx_q = spread(take_map, recv_q.reshape(ctx_count * block_rows, -1), block_rows).reshape(
        tok_dev, -1
    )
    ctx_k = spread(take_map, recv_k.reshape(ctx_count * block_rows, -1), block_rows).reshape(
        tok_dev, -1
    )
    ctx_v = spread(take_map, recv_v.reshape(ctx_count * block_rows, -1), block_rows).reshape(
        tok_dev, -1
    )
    query_four = ctx_q.reshape(tok_dev, groups, per_group, head_dim)

    def visible(key_pos, key_doc):
        return (my_doc[:, None] == key_doc[None, :]) & (key_pos[None, :] <= my_pos[:, None])

    def attend(state, key_blk, value_blk, key_pos, key_doc):
        mask = visible(key_pos, key_doc)

        def attend_run(inner):
            m_old, l_old, accum = inner
            scores = (
                jnp.einsum(
                    "tgqe,sge->gqts", query_four, key_blk, preferred_element_type=jnp.float32
                )
                * scale
            )
            scores = jnp.where(mask[None, None], scores, NEG)
            m_new = jnp.maximum(m_old, jnp.max(scores, axis=-1))
            factor = jnp.exp(m_old - m_new)
            probs = jnp.where(mask[None, None], jnp.exp(scores - m_new[..., None]), 0.0)
            l_new = l_old * factor + jnp.sum(probs, axis=-1)
            accum = accum * factor[..., None] + jnp.einsum(
                "gqts,sge->gqte",
                probs,
                value_blk.astype(jnp.float32),
                precision=lax.Precision.HIGHEST,
                preferred_element_type=jnp.float32,
            )
            return (m_new, l_new, accum)

        return lax.cond(jnp.any(mask), attend_run, lambda inner: inner, state)

    start_state = (
        jnp.full((groups, per_group, tok_dev), NEG, jnp.float32),
        jnp.zeros((groups, per_group, tok_dev), jnp.float32),
        jnp.zeros((groups, per_group, tok_dev, head_dim), jnp.float32),
    )
    grad_four = out_grad.reshape(tok_dev, groups, per_group, head_dim)

    def grads_over(dquery, key_piece, value_piece, start, lse, delta):
        rows = key_piece.shape[0]
        width = math.gcd(rows, 512)

        def grads_one_block(index, inner):
            dq_sum, dk_rows, dv_rows = inner
            offset = index * width
            key_blk = key_piece.reshape(width, groups, head_dim)
            value_blk = value_piece.reshape(width, groups, head_dim)
            key_pos = lax.dynamic_slice_in_dim(ctx_pos, start + offset, width, 0)
            key_doc = lax.dynamic_slice_in_dim(ctx_doc, start + offset, width, 0)
            mask = visible(key_pos, key_doc)

            def one_run(unused):
                scores = (
                    jnp.einsum(
                        "tgqe,sge->gqts", query_four, key_blk, preferred_element_type=jnp.float32
                    )
                    * scale
                )
                weights = jnp.where(mask[None, None], jnp.exp(scores - lse[..., None]), 0.0)
                weights_b = weights.astype(jnp.bfloat16)
                dv_blk = jnp.einsum(
                    "gqts,tgqe->sge", weights_b, grad_four, preferred_element_type=jnp.float32
                )
                dprob = jnp.einsum(
                    "tgqe,sge->gqts", grad_four, value_blk, preferred_element_type=jnp.float32
                )
                dscore = (weights * (dprob - delta[..., None]) * scale).astype(jnp.bfloat16)
                dq_add = jnp.einsum(
                    "gqts,sge->tgqe", dscore, key_blk, preferred_element_type=jnp.float32
                )
                dk_blk = jnp.einsum(
                    "gqts,tgqe->sge", dscore, query_four, preferred_element_type=jnp.float32
                )
                return (dq_add, dk_blk, dv_blk)

            def skip(unused):
                return (
                    jnp.zeros((tok_dev, groups, per_group, head_dim), jnp.float32),
                    jnp.zeros((width, groups, head_dim), jnp.float32),
                    jnp.zeros((width, groups, head_dim), jnp.float32),
                )

            dq_add, dk_blk, dv_blk = lax.cond(jnp.any(mask), one_run, skip, 0)
            dk_rows = dk_blk.reshape(width, groups * head_dim)
            dv_rows = dv_blk.reshape(width, groups * head_dim)
            return (dq_sum + dq_add, dk_rows, dv_rows)

        empty_rows = jnp.zeros((rows, groups * head_dim), jnp.float32)
        return lax.fori_loop(0, rows // width, grads_one_block, (dquery, empty_rows, empty_rows))

    dq_start = jnp.zeros((tok_dev, groups, per_group, head_dim), jnp.float32)
    key_piece = lax.all_gather(ctx_k, "ctx", axis=0, tiled=True)
    value_piece = lax.all_gather(ctx_v, "ctx", axis=0, tiled=True)
    rows = key_piece.shape[0]
    width = math.gcd(rows, 512)

    def fold_one_block(index, inner):
        offset = index * width
        key_blk = lax.dynamic_slice_in_dim(key_piece, offset, width, 0).reshape(
            width, groups, head_dim
        )
        value_blk = lax.dynamic_slice_in_dim(value_piece, offset, width, 0).reshape(
            width, groups, head_dim
        )
        key_pos = lax.dynamic_slice_in_dim(ctx_pos, offset, width, 0)
        key_doc = lax.dynamic_slice_in_dim(ctx_doc, offset, width, 0)
        return attend(inner, key_blk, value_blk, key_pos, key_doc)

    m_end, l_end, accum = lax.fori_loop(0, rows // width, fold_one_block, start_state)
    attn = (accum / l_end[..., None]).astype(jnp.bfloat16)
    attention = attn.transpose(2, 0, 1, 3).reshape(tok_dev, groups * per_group * head_dim)
    lse = m_end + jnp.log(l_end)
    attn_four = attention.reshape(tok_dev, groups, per_group, head_dim)
    delta = jnp.einsum(
        "tgqe,tgqe->gqt", grad_four.astype(jnp.float32), attn_four.astype(jnp.float32)
    )

    def turn(step, inner):
        dquery, key_now, value_now, dk_now, dv_now = inner
        owner = jnp.mod(ctx_rank - step, ctx_count)
        dquery, dk_add, dv_add = grads_over(dquery, key_now, value_now, owner * tok_dev, lse, delta)
        dk_now, dv_now = (
            from_behind((dk_now + dk_add).astype(jnp.bfloat16), "ctx", 1).astype(jnp.float32),
            from_behind((dv_now + dv_add).astype(jnp.bfloat16), "ctx", 1).astype(jnp.float32),
        )
        key_now, value_now = from_behind((key_now, value_now), "ctx", 1)
        return (dquery, key_now, value_now, dk_now, dv_now)

    zero_grads = jnp.zeros((tok_dev, groups * head_dim), jnp.float32)
    dquery, unused_k, unused_v, dkey, dvalue = lax.fori_loop(
        0, ctx_count, turn, (dq_start, ctx_k, ctx_v, zero_grads, zero_grads)
    )
    dq_ctx = dquery.reshape(tok_dev, groups * per_group * head_dim).astype(jnp.bfloat16)
    dk_ctx = dkey.astype(jnp.bfloat16)
    dv_ctx = dvalue.astype(jnp.bfloat16)
    back_map = take_map.T
    home_q, home_k, home_v = (
        lax.all_to_all(
            spread(back_map, dq_ctx, block_rows), "ctx", split_axis=0, concat_axis=0, tiled=True
        ),
        lax.all_to_all(
            spread(back_map, dk_ctx, block_rows), "ctx", split_axis=0, concat_axis=0, tiled=True
        ),
        lax.all_to_all(
            spread(back_map, dv_ctx, block_rows), "ctx", split_axis=0, concat_axis=0, tiled=True
        ),
    )
    pick_map = send_map.T
    dq_loader = spread(pick_map, home_q.reshape(ctx_count * block_rows, -1), block_rows).reshape(
        tok_dev, -1
    )
    dk_loader = spread(pick_map, home_k.reshape(ctx_count * block_rows, -1), block_rows).reshape(
        tok_dev, -1
    )
    dv_loader = spread(pick_map, home_v.reshape(ctx_count * block_rows, -1), block_rows).reshape(
        tok_dev, -1
    )
    grad_terms = (
        transposed_dot(dq_loader, w_query)
        + transposed_dot(dk_loader, w_key)
        + transposed_dot(dv_loader, w_value)
    )
    input_grad = lax.psum_scatter(
        grad_terms.astype(jnp.bfloat16), "heads", scatter_dimension=1, tiled=True
    )
    return (attention, input_grad)


def solution(mesh):
    return jax.shard_map(
        per_device,
        mesh=mesh,
        in_specs=(
            P("ctx", "heads"),
            P(None, "heads"),
            P(None, "heads"),
            P(None, "heads"),
            P(),
            P(),
            P("ctx", "heads"),
        ),
        out_specs=(P("ctx", "heads"), P("ctx", "heads")),
        check_vma=False,
    )
```

profile of v0, /device:TPU:0, one launch (start us, length us, event | category | flops | bytes accessed | tf_op | source)
XLA Modules:
  0.0 553.3 jit_solution(3324979120740839685)
XLA Ops:
  9.7 37.1 %all-gather.4.cloned.1.call-done = bf16[256,8192]{1,0:T(8,128)(2,1)} async-done(((bf16[256,2048]{1,0:T(8,128)(2,1)}), bf16[256,8192]{1,0:T(8,128)(2,1)}) %all-gather.4.cloned.1.call-update) | async-done | bytes 4194320 | tf_op jit(solution)/shard_map/all_gather | solution.py:62
  46.8 4.7 convolution_convert_fusion.13
  52.6 5.5 all-to-all-start.2
  58.1 4.7 convolution_convert_fusion.14
  63.9 3.5 all-to-all-done.2
  67.4 3.6 all-to-all-start
  72.1 11.5 %convolution_convert_fusion.4 = bf16[256,1024]{1,0:T(8,128)(2,1)S(1)} fusion(bf16[256,8192]{1,0:T(8,128)(2,1)} %all-gather.4.cloned.1.call-done, bf16[8192,1024]{1,0:T(8,128)(2,1)} %param.16), kind=kOutput, calls=%fused_computation.45 | convolution fusion | flops 4295229440 | bytes 21495808 | tf_op jit(solution)/shard_map/dot_general | solution.py:64
  85.8 6.0 %all-to-all-start.1 = ((bf16[8,64,1024]{2,1,0:T(8,128)(2,1)}), bf16[8,64,1024]{2,1,0:T(8,128)(2,1)S(1)}, u32[]{:S(2)}, u32[]{:S(2)}) async-start(bf16[8,64,1024]{2,1,0:T(8,128)(2,1)} %copy.107), calls=%async_computation.1 | async-start | bytes 2097152 | tf_op jit(solution)/shard_map/all_to_all | solution.py:77
  98.1 27.5 %all-to-all-done.1 = bf16[8,64,1024]{2,1,0:T(8,128)(2,1)S(1)} async-done(((bf16[8,64,1024]{2,1,0:T(8,128)(2,1)}), bf16[8,64,1024]{2,1,0:T(8,128)(2,1)S(1)}, u32[]{:S(2)}, u32[]{:S(2)}) %all-to-all-start.1) | async-done | bytes 1048608 | tf_op jit(solution)/shard_map/all_to_all | solution.py:77
  129.8 36.9 %all-gather.6.cloned.1.call-done = bf16[2048,256]{1,0:T(8,128)(2,1)} async-done(((bf16[256,256]{1,0:T(8,128)(2,1)}), bf16[2048,256]{1,0:T(8,128)(2,1)}) %all-gather.6.cloned.1.call-update) | async-done | bytes 1048592 | tf_op jit(solution)/shard_map/all_gather | solution.py:188
  166.6 2.3 copy.114
  170.0 47.4 %while.56 = (s32[]{:T(128)}, f32[2,4,256]{2,1,0:T(4,128)S(1)}, f32[2,4,256]{2,1,0:T(4,128)S(1)}, f32[2,4,256,128]{3,2,1,0:T(8,128)}, s32[256]{0:T(256)}, /*index...) while((s32[]{:T(128)}, f32[2,4,256]{2,1,0:T(4,128)S(1)}, ...), condition=%wide.region_10.11_spmd, body=%wide.region_4.10_spmd.sunk | while | flops 1892683776 | bytes 25835900 | solution.py:205
  173.7 8.2 %conditional.5 = ((f32[2,4,256]{2,1,0:T(4,128)S(1)}, f32[2,4,256]{2,1,0:T(4,128)S(1)}, f32[2,4,256,128]{3,2,1,0:T(8,128)})) conditional(s32[]{:T(128)} %convert_element_type.201, (f32[2,4,256]{2,1,0:T(4,128)S(1)}, f32[2,4,256]{2,1,0:T(4,128)S(1)}, f32[2,4,256,128]{3,2,1,0:T(8,128)}) %tuple.116, (pred[256,512]{0,1:T(8,128)(4,1)S(1)}, ...), branch_computations={%region_6.6_spmd, %region_7.9_spmd} | conditional | flops 1892159488 | bytes 25690204 | solution.py:126
  176.6 4.2 fusion.8
  185.5 8.2 %conditional.5 = ((f32[2,4,256]{2,1,0:T(4,128)S(1)}, f32[2,4,256]{2,1,0:T(4,128)S(1)}, f32[2,4,256,128]{3,2,1,0:T(8,128)})) conditional(s32[]{:T(128)} %convert_element_type.201, (f32[2,4,256]{2,1,0:T(4,128)S(1)}, f32[2,4,256]{2,1,0:T(4,128)S(1)}, f32[2,4,256,128]{3,2,1,0:T(8,128)}) %tuple.116, (pred[256,512]{0,1:T(8,128)(4,1)S(1)}, ...), branch_computations={%region_6.6_spmd, %region_7.9_spmd} | conditional | flops 1892159488 | bytes 25690204 | solution.py:126
  188.5 4.2 fusion.8
  197.4 8.2 %conditional.5 = ((f32[2,4,256]{2,1,0:T(4,128)S(1)}, f32[2,4,256]{2,1,0:T(4,128)S(1)}, f32[2,4,256,128]{3,2,1,0:T(8,128)})) conditional(s32[]{:T(128)} %convert_element_type.201, (f32[2,4,256]{2,1,0:T(4,128)S(1)}, f32[2,4,256]{2,1,0:T(4,128)S(1)}, f32[2,4,256,128]{3,2,1,0:T(8,128)}) %tuple.116, (pred[256,512]{0,1:T(8,128)(4,1)S(1)}, ...), branch_computations={%region_6.6_spmd, %region_7.9_spmd} | conditional | flops 1892159488 | bytes 25690204 | solution.py:126
  200.4 4.2 fusion.8
  209.2 8.2 %conditional.5 = ((f32[2,4,256]{2,1,0:T(4,128)S(1)}, f32[2,4,256]{2,1,0:T(4,128)S(1)}, f32[2,4,256,128]{3,2,1,0:T(8,128)})) conditional(s32[]{:T(128)} %convert_element_type.201, (f32[2,4,256]{2,1,0:T(4,128)S(1)}, f32[2,4,256]{2,1,0:T(4,128)S(1)}, f32[2,4,256,128]{3,2,1,0:T(8,128)}) %tuple.116, (pred[256,512]{0,1:T(8,128)(4,1)S(1)}, ...), branch_computations={%region_6.6_spmd, %region_7.9_spmd} | conditional | flops 1892159488 | bytes 25690204 | solution.py:126
  212.2 4.2 fusion.8
  217.4 2.7 fusion.51
  222.4 202.9 %while.57 = (s32[]{:T(128)}, f32[256,2,4,128]{3,0,2,1:T(8,128)S(1)}, bf16[256,256]{1,0:T(8,128)(2,1)}, bf16[256,256]{1,0:T(8,128)(2,1)}, f32[256,256]{0,1:T(8,12...) while((s32[]{:T(128)}, ...), condition=%wide.region_15.16_spmd.clone, body=%wide.region_11.15_spmd.clone.sunk | while | flops 676593664 | bytes 24142468 | solution.py:226
  229.1 2.1 fusion.83
  231.7 5.6 %conditional.6 = (f32[256,2,4,128]{3,0,2,1:T(8,128)S(1)}, f32[256,256]{0,1:T(8,128)S(1)}, f32[256,256]{0,1:T(8,128)S(1)}) conditional(s32[]{:T(128)} %convert_element_type.204, () %tuple.120, (pred[256,256]{0,1:T(8,128)(4,1)}, bf16[256,256]{1,0:T(8,128)(2,1)}, bf16[256,2,4,128]{0,3,2,1:T(8,128)(2,1)}, f32[2,4,256]{2,1,0:T(4,128)}, ...), branch_computations={%region_13.13_spmd, %region_14.14_spmd} | conditional | flops 675282944 | bytes 16203828 | solution.py:179
  240.0 5.5 collective-permute-done.3
  252.9 2.1 fusion.83
  255.6 5.6 %conditional.6 = (f32[256,2,4,128]{3,0,2,1:T(8,128)S(1)}, f32[256,256]{0,1:T(8,128)S(1)}, f32[256,256]{0,1:T(8,128)S(1)}) conditional(s32[]{:T(128)} %convert_element_type.204, () %tuple.120, (pred[256,256]{0,1:T(8,128)(4,1)}, bf16[256,256]{1,0:T(8,128)(2,1)}, bf16[256,2,4,128]{0,3,2,1:T(8,128)(2,1)}, f32[2,4,256]{2,1,0:T(4,128)}, ...), branch_computations={%region_13.13_spmd, %region_14.14_spmd} | conditional | flops 675282944 | bytes 16203828 | solution.py:179
  262.8 2.3 collective-permute-start.2
  265.4 3.6 collective-permute-done.3
  277.3 2.1 fusion.83
  279.9 5.6 %conditional.6 = (f32[256,2,4,128]{3,0,2,1:T(8,128)S(1)}, f32[256,256]{0,1:T(8,128)S(1)}, f32[256,256]{0,1:T(8,128)S(1)}) conditional(s32[]{:T(128)} %convert_element_type.204, () %tuple.120, (pred[256,256]{0,1:T(8,128)(4,1)}, bf16[256,256]{1,0:T(8,128)(2,1)}, bf16[256,2,4,128]{0,3,2,1:T(8,128)(2,1)}, f32[2,4,256]{2,1,0:T(4,128)}, ...), branch_computations={%region_13.13_spmd, %region_14.14_spmd} | conditional | flops 675282944 | bytes 16203828 | solution.py:179
  289.7 3.6 collective-permute-done.3
  293.3 2.5 collective-permute-done.2
  301.4 2.1 fusion.83
  304.1 5.6 %conditional.6 = (f32[256,2,4,128]{3,0,2,1:T(8,128)S(1)}, f32[256,256]{0,1:T(8,128)S(1)}, f32[256,256]{0,1:T(8,128)S(1)}) conditional(s32[]{:T(128)} %convert_element_type.204, () %tuple.120, (pred[256,256]{0,1:T(8,128)(4,1)}, bf16[256,256]{1,0:T(8,128)(2,1)}, bf16[256,2,4,128]{0,3,2,1:T(8,128)(2,1)}, f32[2,4,256]{2,1,0:T(4,128)}, ...), branch_computations={%region_13.13_spmd, %region_14.14_spmd} | conditional | flops 675282944 | bytes 16203828 | solution.py:179
  309.7 2.5 collective-permute-start.3
  314.4 3.0 collective-permute-done.3
  317.4 3.7 collective-permute-done.2
  325.1 2.3 collective-permute-start.1
  328.9 2.1 fusion.83
  331.5 5.6 %conditional.6 = (f32[256,2,4,128]{3,0,2,1:T(8,128)S(1)}, f32[256,256]{0,1:T(8,128)S(1)}, f32[256,256]{0,1:T(8,128)S(1)}) conditional(s32[]{:T(128)} %convert_element_type.204, () %tuple.120, (pred[256,256]{0,1:T(8,128)(4,1)}, bf16[256,256]{1,0:T(8,128)(2,1)}, bf16[256,2,4,128]{0,3,2,1:T(8,128)(2,1)}, f32[2,4,256]{2,1,0:T(4,128)}, ...), branch_computations={%region_13.13_spmd, %region_14.14_spmd} | conditional | flops 675282944 | bytes 16203828 | solution.py:179
  339.2 7.0 %collective-permute-done.3 = bf16[256,256]{0,1:T(8,128)(2,1)S(1)} collective-permute-done((bf16[256,256]{0,1:T(8,128)(2,1)S(1)}, bf16[256,256]{0,1:T(8,128)(2,1)S(1)}, u32[]{:S(2)}, u32[]{:S(2)}) %collective-permute-start.3) | collective-permute-done | bytes 131104 | tf_op jit(solution)/shard_map/while/body/eval_jaxpr/ppermute | solution.py:15
  346.3 2.7 collective-permute-done.2
  354.4 2.1 fusion.83
  357.0 5.6 %conditional.6 = (f32[256,2,4,128]{3,0,2,1:T(8,128)S(1)}, f32[256,256]{0,1:T(8,128)S(1)}, f32[256,256]{0,1:T(8,128)S(1)}) conditional(s32[]{:T(128)} %convert_element_type.204, () %tuple.120, (pred[256,256]{0,1:T(8,128)(4,1)}, bf16[256,256]{1,0:T(8,128)(2,1)}, bf16[256,2,4,128]{0,3,2,1:T(8,128)(2,1)}, f32[2,4,256]{2,1,0:T(4,128)}, ...), branch_computations={%region_13.13_spmd, %region_14.14_spmd} | conditional | flops 675282944 | bytes 16203828 | solution.py:179
  363.7 2.7 collective-permute-start.2
  366.7 4.1 collective-permute-done.3
  381.7 5.6 %conditional.6 = (f32[256,2,4,128]{3,0,2,1:T(8,128)S(1)}, f32[256,256]{0,1:T(8,128)S(1)}, f32[256,256]{0,1:T(8,128)S(1)}) conditional(s32[]{:T(128)} %convert_element_type.204, () %tuple.120, (pred[256,256]{0,1:T(8,128)(4,1)}, bf16[256,256]{1,0:T(8,128)(2,1)}, bf16[256,2,4,128]{0,3,2,1:T(8,128)(2,1)}, f32[2,4,256]{2,1,0:T(4,128)}, ...), branch_computations={%region_13.13_spmd, %region_14.14_spmd} | conditional | flops 675282944 | bytes 16203828 | solution.py:179
  389.0 2.9 collective-permute-start.2
  392.2 4.1 collective-permute-done.3
  401.7 2.3 collective-permute-start.1
  405.5 2.1 fusion.83
  408.2 5.6 %conditional.6 = (f32[256,2,4,128]{3,0,2,1:T(8,128)S(1)}, f32[256,256]{0,1:T(8,128)S(1)}, f32[256,256]{0,1:T(8,128)S(1)}) conditional(s32[]{:T(128)} %convert_element_type.204, () %tuple.120, (pred[256,256]{0,1:T(8,128)(4,1)}, bf16[256,256]{1,0:T(8,128)(2,1)}, bf16[256,2,4,128]{0,3,2,1:T(8,128)(2,1)}, f32[2,4,256]{2,1,0:T(4,128)}, ...), branch_computations={%region_13.13_spmd, %region_14.14_spmd} | conditional | flops 675282944 | bytes 16203828 | solution.py:179
  416.9 6.0 %collective-permute-done.3 = bf16[256,256]{0,1:T(8,128)(2,1)S(1)} collective-permute-done((bf16[256,256]{0,1:T(8,128)(2,1)S(1)}, bf16[256,256]{0,1:T(8,128)(2,1)S(1)}, u32[]{:S(2)}, u32[]{:S(2)}) %collective-permute-start.3) | collective-permute-done | bytes 131104 | tf_op jit(solution)/shard_map/while/body/eval_jaxpr/ppermute | solution.py:15
  426.5 3.4 all-to-all-start.5
  432.1 6.0 %all-to-all-done.5 = bf16[8,64,256]{2,1,0:T(8,128)(2,1)S(1)} async-done(((bf16[8,64,256]{2,1,0:T(8,128)(2,1)}), bf16[8,64,256]{2,1,0:T(8,128)(2,1)S(1)}, u32[]{:S(2)}, u32[]{:S(2)}) %all-to-all-start.5) | async-done | bytes 262176 | tf_op jit(solution)/shard_map/all_to_all | solution.py:240
  438.1 3.6 all-to-all-start.4
  444.8 9.6 %all-to-all-done.4 = bf16[8,64,256]{2,1,0:T(8,128)(2,1)S(1)} async-done(((bf16[8,64,256]{2,1,0:T(8,128)(2,1)}), bf16[8,64,256]{2,1,0:T(8,128)(2,1)S(1)}, u32[]{:S(2)}, u32[]{:S(2)}) %all-to-all-start.4) | async-done | bytes 262176 | tf_op jit(solution)/shard_map/all_to_all | solution.py:237
  454.5 3.6 all-to-all-start.3
  458.7 15.6 %all-to-all-done.3 = bf16[8,64,1024]{2,1,0:T(8,128)(2,1)S(1)} async-done(((bf16[8,64,1024]{2,1,0:T(8,128)(2,1)}), bf16[8,64,1024]{2,1,0:T(8,128)(2,1)S(1)}, u32[]{:S(2)}, u32[]{:S(2)}) %all-to-all-start.3) | async-done | bytes 1048608 | tf_op jit(solution)/shard_map/all_to_all | solution.py:234
  475.3 18.9 %fusion.56 = f32[256,8192]{1,0:T(8,128)} fusion(bf16[256,1024]{1,0:T(8,128)(2,1)S(1)} %bitcast.128, bf16[8192,1024]{1,0:T(8,128)(2,1)} %param.16), kind=kOutput, calls=%fused_computation.91 | convolution fusion | flops 4294967296 | bytes 25690112 | tf_op jit(solution)/shard_map/dot_general | solution.py:43
  494.2 6.1 %convolution_add_fusion.1 = f32[256,8192]{1,0:T(8,128)S(1)} fusion(f32[256,8192]{1,0:T(8,128)} %fusion.56, bf16[256,256]{1,0:T(8,128)(2,1)S(1)} %bitcast.133, bf16[8192,256]{1,0:T(8,128)(2,1)} %param.17), kind=kOutput, calls=%fused_computation.39 | convolution fusion | flops 1075838976 | bytes 21102592 | tf_op jit(solution)/shard_map/dot_general | solution.py:43
  500.3 3.3 fusion.24
  506.2 40.6 %reduce-scatter.2.cloned.1.call-done = bf16[256,2048]{1,0:T(8,128)(2,1)} async-done(((bf16[256,8192]{1,0:T(8,128)(2,1)}), bf16[256,2048]{1,0:T(8,128)(2,1)}) %reduce-scatter.2.cloned.1.call-update) | async-done | bytes 1048592 | tf_op jit(solution)/shard_map/reduce_scatter | solution.py:259
  (327 shorter events, 182.3 us)
Async XLA Ops:
  7.2 39.6 %all-gather.4.cloned.1.call-start = ((), (), s32[]{:S(2)}) async-start(), calls=%async_computation.7 | async-start | bytes 5242880 | tf_op jit(solution)/shard_map/all_gather | solution.py:62
  8.6 75.0 %copy-start.6 = (s32[4]{0:T(128)}, s32[4]{0:T(128)S(1)}, u32[]{:S(2)}) copy-start(s32[4]{0:T(128)S(1)} %dynamic_slice.75) | copy-start | bytes 52
  9.7 115.9 %copy-start.8 = (s32[4]{0:T(128)}, s32[4]{0:T(128)S(1)}, u32[]{:S(2)}) copy-start(s32[4]{0:T(128)S(1)} %and_select_fusion) | copy-start | bytes 52
  52.6 14.8 %all-to-all-start.2 = ((bf16[8,64,256]{2,1,0:T(8,128)(2,1)}), bf16[8,64,256]{2,1,0:T(8,128)(2,1)S(1)}, u32[]{:S(2)}, u32[]{:S(2)}) async-start(bf16[8,64,256]{2,1,0:T(8,128)(2,1)} %copy.111), calls=%async_computation.2 | async-start | bytes 524288 | tf_op jit(solution)/shard_map/all_to_all | solution.py:83
  67.4 18.4 %all-to-all-start = ((bf16[8,64,256]{2,1,0:T(8,128)(2,1)}), bf16[8,64,256]{2,1,0:T(8,128)(2,1)S(1)}, u32[]{:S(2)}, u32[]{:S(2)}) async-start(bf16[8,64,256]{2,1,0:T(8,128)(2,1)} %copy.103), calls=%async_computation | async-start | bytes 524288 | tf_op jit(solution)/shard_map/all_to_all | solution.py:80
  71.0 57.1 %all-gather.8.cloned.1.call-start = ((), (), s32[]{:S(2)}) async-start(), calls=%async_computation.9 | async-start | bytes 1179648 | tf_op jit(solution)/shard_map/all_gather | solution.py:189
  83.6 9.2 %copy-start.10 = (s32[8]{0:T(128)S(1)}, s32[8]{0:T(128)}, u32[]{:S(2)}) copy-start(s32[8]{0:T(128)} %param.19) | copy-start | bytes 100
  83.6 14.2 %copy-start.5 = (bf16[256,1024]{1,0:T(8,128)(2,1)S(1)}, bf16[256,1024]{1,0:T(8,128)(2,1)}, u32[]{:S(2)}) copy-start(bf16[256,1024]{1,0:T(8,128)(2,1)} %param.21) | copy-start | bytes 1572868
  85.8 39.7 %all-to-all-start.1 = ((bf16[8,64,1024]{2,1,0:T(8,128)(2,1)}), bf16[8,64,1024]{2,1,0:T(8,128)(2,1)S(1)}, u32[]{:S(2)}, u32[]{:S(2)}) async-start(bf16[8,64,1024]{2,1,0:T(8,128)(2,1)} %copy.107), calls=%async_computation.1 | async-start | bytes 2097152 | tf_op jit(solution)/shard_map/all_to_all | solution.py:77
  91.8 74.8 %all-gather.6.cloned.1.call-start = ((), (), s32[]{:S(2)}) async-start(), calls=%async_computation.8 | async-start | bytes 1179648 | tf_op jit(solution)/shard_map/all_gather | solution.py:188
  174.7 2.0 copy-start.1
  180.9 1.0 copy-start.2
  186.5 2.0 copy-start.1
  198.4 2.0 copy-start.1
  204.6 1.0 copy-start.2
  210.3 2.0 copy-start.1
  222.4 203.0 %copy-start.9 = (s32[4]{0:T(128)S(1)}, s32[4]{0:T(128)}, u32[]{:S(2)}) copy-start(s32[4]{0:T(128)} %copy-done.8) | copy-start | bytes 52
  224.0 23.6 %collective-permute-start = (bf16[256,256]{1,0:T(8,128)(2,1)}, bf16[256,256]{1,0:T(8,128)(2,1)}, u32[]{:S(2)}, u32[]{:S(2)}) collective-permute-start(bf16[256,256]{1,0:T(8,128)(2,1)} %copy.227), channel_id=1, source_target_pairs={{0,4},{4,8},{8,12},{12,16},{16,20},{20,24},{24,28},{28,0},{1,5},{5... | collective-permute-start | bytes 393224 | tf_op jit(solution)/shard_map/while/body/eval_jaxpr/ppermute | solution.py:15
  226.1 21.5 %collective-permute-start.1 = (bf16[256,256]{1,0:T(8,128)(2,1)}, bf16[256,256]{1,0:T(8,128)(2,1)}, u32[]{:S(2)}, u32[]{:S(2)}) collective-permute-start(bf16[256,256]{1,0:T(8,128)(2,1)} %copy.228), channel_id=1, source_target_pairs={{0,4},{4,8},{8,12},{12,16},{16,20},{20,24},{24,28},{28,0},{1,5},{5... | collective-permute-start | bytes 393224 | tf_op jit(solution)/shard_map/while/body/eval_jaxpr/ppermute | solution.py:15
  233.6 2.6 copy-start
  237.3 8.2 %collective-permute-start.3 = (bf16[256,256]{0,1:T(8,128)(2,1)S(1)}, bf16[256,256]{0,1:T(8,128)(2,1)S(1)}, u32[]{:S(2)}, u32[]{:S(2)}) collective-permute-start(bf16[256,256]{0,1:T(8,128)(2,1)S(1)} %fusion.85), channel_id=1, source_target_pairs={{0,4},{4,8},{8,12},{12,16},{16,20},{20,24},{24,28},{28,0},{1,5},{5... | collective-permute-start | bytes 393224 | tf_op jit(solution)/shard_map/while/body/eval_jaxpr/ppermute | solution.py:15
  238.0 8.9 %collective-permute-start.2 = (bf16[256,256]{0,1:T(8,128)(2,1)S(1)}, bf16[256,256]{0,1:T(8,128)(2,1)S(1)}, u32[]{:S(2)}, u32[]{:S(2)}) collective-permute-start(bf16[256,256]{0,1:T(8,128)(2,1)S(1)} %fusion.84), channel_id=1, source_target_pairs={{0,4},{4,8},{8,12},{12,16},{16,20},{20,24},{24,28},{28,0},{1,5},{5... | collective-permute-start | bytes 393224 | tf_op jit(solution)/shard_map/while/body/eval_jaxpr/ppermute | solution.py:15
  249.2 22.0 %collective-permute-start = (bf16[256,256]{1,0:T(8,128)(2,1)}, bf16[256,256]{1,0:T(8,128)(2,1)}, u32[]{:S(2)}, u32[]{:S(2)}) collective-permute-start(bf16[256,256]{1,0:T(8,128)(2,1)} %copy.227), channel_id=1, source_target_pairs={{0,4},{4,8},{8,12},{12,16},{16,20},{20,24},{24,28},{28,0},{1,5},{5... | collective-permute-start | bytes 393224 | tf_op jit(solution)/shard_map/while/body/eval_jaxpr/ppermute | solution.py:15
  250.8 20.4 %collective-permute-start.1 = (bf16[256,256]{1,0:T(8,128)(2,1)}, bf16[256,256]{1,0:T(8,128)(2,1)}, u32[]{:S(2)}, u32[]{:S(2)}) collective-permute-start(bf16[256,256]{1,0:T(8,128)(2,1)} %copy.228), channel_id=1, source_target_pairs={{0,4},{4,8},{8,12},{12,16},{16,20},{20,24},{24,28},{28,0},{1,5},{5... | collective-permute-start | bytes 393224 | tf_op jit(solution)/shard_map/while/body/eval_jaxpr/ppermute | solution.py:15
  257.5 2.6 copy-start
  261.2 7.7 %collective-permute-start.3 = (bf16[256,256]{0,1:T(8,128)(2,1)S(1)}, bf16[256,256]{0,1:T(8,128)(2,1)S(1)}, u32[]{:S(2)}, u32[]{:S(2)}) collective-permute-start(bf16[256,256]{0,1:T(8,128)(2,1)S(1)} %fusion.85), channel_id=1, source_target_pairs={{0,4},{4,8},{8,12},{12,16},{16,20},{20,24},{24,28},{28,0},{1,5},{5... | collective-permute-start | bytes 393224 | tf_op jit(solution)/shard_map/while/body/eval_jaxpr/ppermute | solution.py:15
  262.8 7.7 %collective-permute-start.2 = (bf16[256,256]{0,1:T(8,128)(2,1)S(1)}, bf16[256,256]{0,1:T(8,128)(2,1)S(1)}, u32[]{:S(2)}, u32[]{:S(2)}) collective-permute-start(bf16[256,256]{0,1:T(8,128)(2,1)S(1)} %fusion.84), channel_id=1, source_target_pairs={{0,4},{4,8},{8,12},{12,16},{16,20},{20,24},{24,28},{28,0},{1,5},{5... | collective-permute-start | bytes 393224 | tf_op jit(solution)/shard_map/while/body/eval_jaxpr/ppermute | solution.py:15
  272.8 23.7 %collective-permute-start = (bf16[256,256]{1,0:T(8,128)(2,1)}, bf16[256,256]{1,0:T(8,128)(2,1)}, u32[]{:S(2)}, u32[]{:S(2)}) collective-permute-start(bf16[256,256]{1,0:T(8,128)(2,1)} %copy.227), channel_id=1, source_target_pairs={{0,4},{4,8},{8,12},{12,16},{16,20},{20,24},{24,28},{28,0},{1,5},{5... | collective-permute-start | bytes 393224 | tf_op jit(solution)/shard_map/while/body/eval_jaxpr/ppermute | solution.py:15
  274.4 22.1 %collective-permute-start.1 = (bf16[256,256]{1,0:T(8,128)(2,1)}, bf16[256,256]{1,0:T(8,128)(2,1)}, u32[]{:S(2)}, u32[]{:S(2)}) collective-permute-start(bf16[256,256]{1,0:T(8,128)(2,1)} %copy.228), channel_id=1, source_target_pairs={{0,4},{4,8},{8,12},{12,16},{16,20},{20,24},{24,28},{28,0},{1,5},{5... | collective-permute-start | bytes 393224 | tf_op jit(solution)/shard_map/while/body/eval_jaxpr/ppermute | solution.py:15
  281.8 2.6 copy-start
  285.5 7.7 %collective-permute-start.3 = (bf16[256,256]{0,1:T(8,128)(2,1)S(1)}, bf16[256,256]{0,1:T(8,128)(2,1)S(1)}, u32[]{:S(2)}, u32[]{:S(2)}) collective-permute-start(bf16[256,256]{0,1:T(8,128)(2,1)S(1)} %fusion.85), channel_id=1, source_target_pairs={{0,4},{4,8},{8,12},{12,16},{16,20},{20,24},{24,28},{28,0},{1,5},{5... | collective-permute-start | bytes 393224 | tf_op jit(solution)/shard_map/while/body/eval_jaxpr/ppermute | solution.py:15
  288.0 7.7 %collective-permute-start.2 = (bf16[256,256]{0,1:T(8,128)(2,1)S(1)}, bf16[256,256]{0,1:T(8,128)(2,1)S(1)}, u32[]{:S(2)}, u32[]{:S(2)}) collective-permute-start(bf16[256,256]{0,1:T(8,128)(2,1)S(1)} %fusion.84), channel_id=1, source_target_pairs={{0,4},{4,8},{8,12},{12,16},{16,20},{20,24},{24,28},{28,0},{1,5},{5... | collective-permute-start | bytes 393224 | tf_op jit(solution)/shard_map/while/body/eval_jaxpr/ppermute | solution.py:15
  298.1 23.9 %collective-permute-start = (bf16[256,256]{1,0:T(8,128)(2,1)}, bf16[256,256]{1,0:T(8,128)(2,1)}, u32[]{:S(2)}, u32[]{:S(2)}) collective-permute-start(bf16[256,256]{1,0:T(8,128)(2,1)} %copy.227), channel_id=1, source_target_pairs={{0,4},{4,8},{8,12},{12,16},{16,20},{20,24},{24,28},{28,0},{1,5},{5... | collective-permute-start | bytes 393224 | tf_op jit(solution)/shard_map/while/body/eval_jaxpr/ppermute | solution.py:15
  299.6 22.3 %collective-permute-start.1 = (bf16[256,256]{1,0:T(8,128)(2,1)}, bf16[256,256]{1,0:T(8,128)(2,1)}, u32[]{:S(2)}, u32[]{:S(2)}) collective-permute-start(bf16[256,256]{1,0:T(8,128)(2,1)} %copy.228), channel_id=1, source_target_pairs={{0,4},{4,8},{8,12},{12,16},{16,20},{20,24},{24,28},{28,0},{1,5},{5... | collective-permute-start | bytes 393224 | tf_op jit(solution)/shard_map/while/body/eval_jaxpr/ppermute | solution.py:15
  306.0 2.6 copy-start
  309.7 7.7 %collective-permute-start.3 = (bf16[256,256]{0,1:T(8,128)(2,1)S(1)}, bf16[256,256]{0,1:T(8,128)(2,1)S(1)}, u32[]{:S(2)}, u32[]{:S(2)}) collective-permute-start(bf16[256,256]{0,1:T(8,128)(2,1)S(1)} %fusion.85), channel_id=1, source_target_pairs={{0,4},{4,8},{8,12},{12,16},{16,20},{20,24},{24,28},{28,0},{1,5},{5... | collective-permute-start | bytes 393224 | tf_op jit(solution)/shard_map/while/body/eval_jaxpr/ppermute | solution.py:15
  313.2 8.0 %collective-permute-start.2 = (bf16[256,256]{0,1:T(8,128)(2,1)S(1)}, bf16[256,256]{0,1:T(8,128)(2,1)S(1)}, u32[]{:S(2)}, u32[]{:S(2)}) collective-permute-start(bf16[256,256]{0,1:T(8,128)(2,1)S(1)} %fusion.84), channel_id=1, source_target_pairs={{0,4},{4,8},{8,12},{12,16},{16,20},{20,24},{24,28},{28,0},{1,5},{5... | collective-permute-start | bytes 393224 | tf_op jit(solution)/shard_map/while/body/eval_jaxpr/ppermute | solution.py:15
  323.5 26.3 %collective-permute-start = (bf16[256,256]{1,0:T(8,128)(2,1)}, bf16[256,256]{1,0:T(8,128)(2,1)}, u32[]{:S(2)}, u32[]{:S(2)}) collective-permute-start(bf16[256,256]{1,0:T(8,128)(2,1)} %copy.227), channel_id=1, source_target_pairs={{0,4},{4,8},{8,12},{12,16},{16,20},{20,24},{24,28},{28,0},{1,5},{5... | collective-permute-start | bytes 393224 | tf_op jit(solution)/shard_map/while/body/eval_jaxpr/ppermute | solution.py:15
  325.1 24.7 %collective-permute-start.1 = (bf16[256,256]{1,0:T(8,128)(2,1)}, bf16[256,256]{1,0:T(8,128)(2,1)}, u32[]{:S(2)}, u32[]{:S(2)}) collective-permute-start(bf16[256,256]{1,0:T(8,128)(2,1)} %copy.228), channel_id=1, source_target_pairs={{0,4},{4,8},{8,12},{12,16},{16,20},{20,24},{24,28},{28,0},{1,5},{5... | collective-permute-start | bytes 393224 | tf_op jit(solution)/shard_map/while/body/eval_jaxpr/ppermute | solution.py:15
  333.4 2.6 copy-start
  337.2 9.1 %collective-permute-start.3 = (bf16[256,256]{0,1:T(8,128)(2,1)S(1)}, bf16[256,256]{0,1:T(8,128)(2,1)S(1)}, u32[]{:S(2)}, u32[]{:S(2)}) collective-permute-start(bf16[256,256]{0,1:T(8,128)(2,1)S(1)} %fusion.85), channel_id=1, source_target_pairs={{0,4},{4,8},{8,12},{12,16},{16,20},{20,24},{24,28},{28,0},{1,5},{5... | collective-permute-start | bytes 393224 | tf_op jit(solution)/shard_map/while/body/eval_jaxpr/ppermute | solution.py:15
  338.8 10.2 %collective-permute-start.2 = (bf16[256,256]{0,1:T(8,128)(2,1)S(1)}, bf16[256,256]{0,1:T(8,128)(2,1)S(1)}, u32[]{:S(2)}, u32[]{:S(2)}) collective-permute-start(bf16[256,256]{0,1:T(8,128)(2,1)S(1)} %fusion.84), channel_id=1, source_target_pairs={{0,4},{4,8},{8,12},{12,16},{16,20},{20,24},{24,28},{28,0},{1,5},{5... | collective-permute-start | bytes 393224 | tf_op jit(solution)/shard_map/while/body/eval_jaxpr/ppermute | solution.py:15
  351.3 21.6 %collective-permute-start = (bf16[256,256]{1,0:T(8,128)(2,1)}, bf16[256,256]{1,0:T(8,128)(2,1)}, u32[]{:S(2)}, u32[]{:S(2)}) collective-permute-start(bf16[256,256]{1,0:T(8,128)(2,1)} %copy.227), channel_id=1, source_target_pairs={{0,4},{4,8},{8,12},{12,16},{16,20},{20,24},{24,28},{28,0},{1,5},{5... | collective-permute-start | bytes 393224 | tf_op jit(solution)/shard_map/while/body/eval_jaxpr/ppermute | solution.py:15
  352.9 20.1 %collective-permute-start.1 = (bf16[256,256]{1,0:T(8,128)(2,1)}, bf16[256,256]{1,0:T(8,128)(2,1)}, u32[]{:S(2)}, u32[]{:S(2)}) collective-permute-start(bf16[256,256]{1,0:T(8,128)(2,1)} %copy.228), channel_id=1, source_target_pairs={{0,4},{4,8},{8,12},{12,16},{16,20},{20,24},{24,28},{28,0},{1,5},{5... | collective-permute-start | bytes 393224 | tf_op jit(solution)/shard_map/while/body/eval_jaxpr/ppermute | solution.py:15
  358.9 2.6 copy-start
  362.7 8.1 %collective-permute-start.3 = (bf16[256,256]{0,1:T(8,128)(2,1)S(1)}, bf16[256,256]{0,1:T(8,128)(2,1)S(1)}, u32[]{:S(2)}, u32[]{:S(2)}) collective-permute-start(bf16[256,256]{0,1:T(8,128)(2,1)S(1)} %fusion.85), channel_id=1, source_target_pairs={{0,4},{4,8},{8,12},{12,16},{16,20},{20,24},{24,28},{28,0},{1,5},{5... | collective-permute-start | bytes 393224 | tf_op jit(solution)/shard_map/while/body/eval_jaxpr/ppermute | solution.py:15
  363.7 8.5 %collective-permute-start.2 = (bf16[256,256]{0,1:T(8,128)(2,1)S(1)}, bf16[256,256]{0,1:T(8,128)(2,1)S(1)}, u32[]{:S(2)}, u32[]{:S(2)}) collective-permute-start(bf16[256,256]{0,1:T(8,128)(2,1)S(1)} %fusion.84), channel_id=1, source_target_pairs={{0,4},{4,8},{8,12},{12,16},{16,20},{20,24},{24,28},{28,0},{1,5},{5... | collective-permute-start | bytes 393224 | tf_op jit(solution)/shard_map/while/body/eval_jaxpr/ppermute | solution.py:15
  374.5 24.0 %collective-permute-start = (bf16[256,256]{1,0:T(8,128)(2,1)}, bf16[256,256]{1,0:T(8,128)(2,1)}, u32[]{:S(2)}, u32[]{:S(2)}) collective-permute-start(bf16[256,256]{1,0:T(8,128)(2,1)} %copy.227), channel_id=1, source_target_pairs={{0,4},{4,8},{8,12},{12,16},{16,20},{20,24},{24,28},{28,0},{1,5},{5... | collective-permute-start | bytes 393224 | tf_op jit(solution)/shard_map/while/body/eval_jaxpr/ppermute | solution.py:15
  376.1 22.5 %collective-permute-start.1 = (bf16[256,256]{1,0:T(8,128)(2,1)}, bf16[256,256]{1,0:T(8,128)(2,1)}, u32[]{:S(2)}, u32[]{:S(2)}) collective-permute-start(bf16[256,256]{1,0:T(8,128)(2,1)} %copy.228), channel_id=1, source_target_pairs={{0,4},{4,8},{8,12},{12,16},{16,20},{20,24},{24,28},{28,0},{1,5},{5... | collective-permute-start | bytes 393224 | tf_op jit(solution)/shard_map/while/body/eval_jaxpr/ppermute | solution.py:15
  383.6 2.6 copy-start
  387.3 9.0 %collective-permute-start.3 = (bf16[256,256]{0,1:T(8,128)(2,1)S(1)}, bf16[256,256]{0,1:T(8,128)(2,1)S(1)}, u32[]{:S(2)}, u32[]{:S(2)}) collective-permute-start(bf16[256,256]{0,1:T(8,128)(2,1)S(1)} %fusion.85), channel_id=1, source_target_pairs={{0,4},{4,8},{8,12},{12,16},{16,20},{20,24},{24,28},{28,0},{1,5},{5... | collective-permute-start | bytes 393224 | tf_op jit(solution)/shard_map/while/body/eval_jaxpr/ppermute | solution.py:15
  389.0 8.8 %collective-permute-start.2 = (bf16[256,256]{0,1:T(8,128)(2,1)S(1)}, bf16[256,256]{0,1:T(8,128)(2,1)S(1)}, u32[]{:S(2)}, u32[]{:S(2)}) collective-permute-start(bf16[256,256]{0,1:T(8,128)(2,1)S(1)} %fusion.84), channel_id=1, source_target_pairs={{0,4},{4,8},{8,12},{12,16},{16,20},{20,24},{24,28},{28,0},{1,5},{5... | collective-permute-start | bytes 393224 | tf_op jit(solution)/shard_map/while/body/eval_jaxpr/ppermute | solution.py:15
  400.1 25.2 %collective-permute-start = (bf16[256,256]{1,0:T(8,128)(2,1)}, bf16[256,256]{1,0:T(8,128)(2,1)}, u32[]{:S(2)}, u32[]{:S(2)}) collective-permute-start(bf16[256,256]{1,0:T(8,128)(2,1)} %copy.227), channel_id=1, source_target_pairs={{0,4},{4,8},{8,12},{12,16},{16,20},{20,24},{24,28},{28,0},{1,5},{5... | collective-permute-start | bytes 393224 | tf_op jit(solution)/shard_map/while/body/eval_jaxpr/ppermute | solution.py:15
  401.7 23.6 %collective-permute-start.1 = (bf16[256,256]{1,0:T(8,128)(2,1)}, bf16[256,256]{1,0:T(8,128)(2,1)}, u32[]{:S(2)}, u32[]{:S(2)}) collective-permute-start(bf16[256,256]{1,0:T(8,128)(2,1)} %copy.228), channel_id=1, source_target_pairs={{0,4},{4,8},{8,12},{12,16},{16,20},{20,24},{24,28},{28,0},{1,5},{5... | collective-permute-start | bytes 393224 | tf_op jit(solution)/shard_map/while/body/eval_jaxpr/ppermute | solution.py:15
  410.1 2.6 copy-start
  413.8 9.0 %collective-permute-start.3 = (bf16[256,256]{0,1:T(8,128)(2,1)S(1)}, bf16[256,256]{0,1:T(8,128)(2,1)S(1)}, u32[]{:S(2)}, u32[]{:S(2)}) collective-permute-start(bf16[256,256]{0,1:T(8,128)(2,1)S(1)} %fusion.85), channel_id=1, source_target_pairs={{0,4},{4,8},{8,12},{12,16},{16,20},{20,24},{24,28},{28,0},{1,5},{5... | collective-permute-start | bytes 393224 | tf_op jit(solution)/shard_map/while/body/eval_jaxpr/ppermute | solution.py:15
  415.2 9.4 %collective-permute-start.2 = (bf16[256,256]{0,1:T(8,128)(2,1)S(1)}, bf16[256,256]{0,1:T(8,128)(2,1)S(1)}, u32[]{:S(2)}, u32[]{:S(2)}) collective-permute-start(bf16[256,256]{0,1:T(8,128)(2,1)S(1)} %fusion.84), channel_id=1, source_target_pairs={{0,4},{4,8},{8,12},{12,16},{16,20},{20,24},{24,28},{28,0},{1,5},{5... | collective-permute-start | bytes 393224 | tf_op jit(solution)/shard_map/while/body/eval_jaxpr/ppermute | solution.py:15
  426.5 11.6 %all-to-all-start.5 = ((bf16[8,64,256]{2,1,0:T(8,128)(2,1)}), bf16[8,64,256]{2,1,0:T(8,128)(2,1)S(1)}, u32[]{:S(2)}, u32[]{:S(2)}) async-start(bf16[8,64,256]{2,1,0:T(8,128)(2,1)} %copy.132), calls=%async_computation.5 | async-start | bytes 524288 | tf_op jit(solution)/shard_map/all_to_all | solution.py:240
  438.1 16.4 %all-to-all-start.4 = ((bf16[8,64,256]{2,1,0:T(8,128)(2,1)}), bf16[8,64,256]{2,1,0:T(8,128)(2,1)S(1)}, u32[]{:S(2)}, u32[]{:S(2)}) async-start(bf16[8,64,256]{2,1,0:T(8,128)(2,1)} %copy.127), calls=%async_computation.4 | async-start | bytes 524288 | tf_op jit(solution)/shard_map/all_to_all | solution.py:237
  441.8 16.3 %copy-start.7 = (s32[4]{0:T(128)S(1)}, s32[4]{0:T(128)}, u32[]{:S(2)}) copy-start(s32[4]{0:T(128)} %copy-done.6) | copy-start | bytes 52
  454.5 19.9 %all-to-all-start.3 = ((bf16[8,64,1024]{2,1,0:T(8,128)(2,1)}), bf16[8,64,1024]{2,1,0:T(8,128)(2,1)S(1)}, u32[]{:S(2)}, u32[]{:S(2)}) async-start(bf16[8,64,1024]{2,1,0:T(8,128)(2,1)} %copy.122), calls=%async_computation.3 | async-start | bytes 2097152 | tf_op jit(solution)/shard_map/all_to_all | solution.py:234
  458.0 88.7 %reduce-scatter.2.cloned.1.call-start = ((), (), s32[]{:S(2)}) async-start(), calls=%async_computation.10 | async-start | bytes 5242880 | tf_op jit(solution)/shard_map/reduce_scatter | solution.py:259
  494.2 6.1 %copy-start.3 = (bf16[8192,256]{1,0:T(8,128)(2,1)S(1)}, bf16[8192,256]{1,0:T(8,128)(2,1)}, u32[]{:S(2)}) copy-start(bf16[8192,256]{1,0:T(8,128)(2,1)} %param.18) | copy-start | bytes 12582916
  503.6 1.0 copy-start.4
  (2 other events, 1.9 us)
Sparse Core Ops, SparseCore 0:
  9.6 37.1 all-gather.3
  74.0 51.0 all-gather.7
  127.2 39.3 all-gather.5
  503.7 43.0 reduce-scatter.1
where the time goes:
time: 556 us; the launch traced here: 553 us
  waiting for transfers between devices  231 us (42%)
  matrix products  104 us (19%)
  local copies, waits for them, and re-layouts  90.9 us (16%)
  starting transfers between devices  56.4 us (10%)
  other arithmetic  49 us (9%)
  between operations  14.1 us (3%)
  loops' own time  8.15 us (1%)
    ppermute x32, waiting for transfers between devices, from_behind(): return lax.ppermute(value, axis, pairs)  53.3 us
    reduce_scatter x1, waiting for transfers between devices, per_device(): lax.psum_scatter(grad_terms.astype(jnp.bfloat16), 'heads', scatter_dimens...  40.6 us
    all_gather x1, waiting for transfers between devices, per_device(): piece = lax.all_gather(activations, 'heads', axis=1, tiled=True)  37.1 us
    all_gather x1, waiting for transfers between devices, per_device(): key_piece = lax.all_gather(ctx_k, 'ctx', axis=0, tiled=True)  36.9 us
    ppermute x32, starting transfers between devices, from_behind(): return lax.ppermute(value, axis, pairs)  30.5 us
    dot_general x3, matrix products, transposed_dot(): lax.dot_general(left, weight, (((1,), (1,)), ((), ())), preferred_element...  28.3 us
    all_to_all x1, waiting for transfers between devices, per_device(): lax.all_to_all(spread(send_map, loader_q, block_rows), 'ctx', split_axis=...  27.5 us
    while x16, local copies, waits for them, and re-layouts  25 us
  transfers between devices with their start and end apart: 42, of which 24 were waited for; matrix products, arithmetic and copies ran while one was open for 25% of the time, Pallas kernels for 0%

commit v1 on v0

--- a/solution.py
+++ b/solution.py
@@ -3,6 +3,7 @@
 import jax.numpy as jnp
 from jax import lax
 from jax.sharding import PartitionSpec as P
+from jax.lax import axis_index, axis_size, ppermute
 
 HD = 128
 QPK = 4
@@ -185,7 +186,21 @@
         return lax.fori_loop(0, rows // width, grads_one_block, (dquery, empty_rows, empty_rows))
 
     dq_start = jnp.zeros((tok_dev, groups, per_group, head_dim), jnp.float32)
-    key_piece = lax.all_gather(ctx_k, "ctx", axis=0, tiled=True)
+
+    def sector_place(body):
+        lanes = axis_size("ctx")
+        z2 = sorted(((j, (j + 1) % lanes) for j in range(lanes)))
+        heard = body
+        trail = [heard]
+        for j0 in range(1, lanes):
+            heard = ppermute(heard, "ctx", z2)
+            trail.insert(0, heard)
+        piece_next = jnp.concatenate(trail, axis=0)
+        newest = axis_index("ctx") + 1
+        tmp = jnp.roll(piece_next, shift=newest * body.shape[0], axis=0)
+        return tmp
+
+    key_piece = sector_place(ctx_k)
     value_piece = lax.all_gather(ctx_v, "ctx", axis=0, tiled=True)
     rows = key_piece.shape[0]
     width = math.gcd(rows, 512)

time: 556 us -> 562 us (1.011)
  waiting for transfers between devices: 231 us -> 222 us
  local copies, waits for them, and re-layouts: 90.9 us -> 97.3 us
  starting transfers between devices: 56.4 us -> 62.2 us
    all_gather x1 -> x0, waiting for transfers between devices: 36.9 us -> none  [per_device(): key_piece = lax.all_gather(ctx_k, 'ctx', axis=0, tiled=True)]
    ppermute x0 -> x7, waiting for transfers between devices: none -> 20 us  [sector_place(): heard = ppermute(heard, 'ctx', z2)]
    all_gather x1, waiting for transfers between devices: 0.02 us -> 16.3 us  [per_device(): value_piece = lax.all_gather(ctx_v, 'ctx', axis=0, tiled=True)]
    all_to_all x1, waiting for transfers between devices: 27.5 us -> 12.6 us  [per_device(): lax.all_to_all(spread(send_map, loader_q, block_rows), 'ctx', split_axis=...]
    all_to_all x1, waiting for transfers between devices: 0.01 us -> 8.93 us  [per_device(): lax.all_to_all(spread(send_map, loader_k, block_rows), 'ctx', split_axis=...]
  transfers between devices with their start and end apart: 42 -> 48, of which waited for: 24 -> 30; matrix products, arithmetic and copies ran while one was open for 25% -> 26% of each run, Pallas kernels for 0% -> 0%
where the time goes in v1:
time: 562 us; the launch traced here: 559 us
  waiting for transfers between devices  222 us (40%)
  matrix products  105 us (19%)
  local copies, waits for them, and re-layouts  97.3 us (17%)
  starting transfers between devices  62.2 us (11%)
  other arithmetic  48.4 us (9%)
  between operations  14.2 us (3%)
  loops' own time  9.13 us (2%)
    ppermute x32, waiting for transfers between devices, from_behind(): return lax.ppermute(value, axis, pairs)  53.5 us
    reduce_scatter x1, waiting for transfers between devices, per_device(): lax.psum_scatter(grad_terms.astype(jnp.bfloat16), 'heads', scatter_dimens...  40.4 us
    all_gather x1, waiting for transfers between devices, per_device(): piece = lax.all_gather(activations, 'heads', axis=1, tiled=True)  38.1 us
    ppermute x32, starting transfers between devices, from_behind(): return lax.ppermute(value, axis, pairs)  30.4 us
    dot_general x3, matrix products, transposed_dot(): lax.dot_general(left, weight, (((1,), (1,)), ((), ())), preferred_element...  28.6 us
    while x16, local copies, waits for them, and re-layouts  25.2 us
    ppermute x7, waiting for transfers between devices, sector_place(): heard = ppermute(heard, 'ctx', z2)  20 us
    dot_general x4, matrix products, attend_run(): jnp.einsum('gqts,sge->gqte', probs, value_blk.astype(jnp.float32), precis...  16.8 us
  transfers between devices with their start and end apart: 48, of which 30 were waited for; matrix products, arithmetic and copies ran while one was open for 26% of the time, Pallas kernels for 0%

profile of v1, /device:TPU:0, one launch (start us, length us, event | category | flops | bytes accessed | tf_op | source)
XLA Modules:
  0.0 559.0 jit_solution(11764167370304066795)
XLA Ops:
  8.6 38.1 %all-gather.3.cloned.1.call-done = bf16[256,8192]{1,0:T(8,128)(2,1)} async-done(((bf16[256,2048]{1,0:T(8,128)(2,1)}), bf16[256,8192]{1,0:T(8,128)(2,1)}) %all-gather.3.cloned.1.call-update) | async-done | bytes 4194320 | tf_op jit(solution)/shard_map/all_gather | solution.py:63
  46.8 4.7 convolution_convert_fusion.14
  52.6 5.5 all-to-all-start
  58.5 8.9 %all-to-all-done = bf16[8,64,256]{2,1,0:T(8,128)(2,1)S(1)} async-done(((bf16[8,64,256]{2,1,0:T(8,128)(2,1)}), bf16[8,64,256]{2,1,0:T(8,128)(2,1)S(1)}, u32[]{:S(2)}, u32[]{:S(2)}) %all-to-all-start) | async-done | bytes 262176 | tf_op jit(solution)/shard_map/all_to_all | solution.py:81
  69.8 6.5 %collective-permute-done.4 = bf16[256,256]{1,0:T(8,128)(2,1)S(1)} collective-permute-done((bf16[256,256]{1,0:T(8,128)(2,1)}, bf16[256,256]{1,0:T(8,128)(2,1)S(1)}, u32[]{:S(2)}, u32[]{:S(2)}) %collective-permute-start.4) | collective-permute-done | bytes 131104 | tf_op jit(solution)/shard_map/ppermute | solution.py:196
  81.4 2.6 collective-permute-done.5
  83.9 4.7 convolution_convert_fusion.13
  88.7 2.9 collective-permute-done.6
  92.7 6.0 %all-to-all-start.2 = ((bf16[8,64,256]{2,1,0:T(8,128)(2,1)}), bf16[8,64,256]{2,1,0:T(8,128)(2,1)S(1)}, u32[]{:S(2)}, u32[]{:S(2)}) async-start(bf16[8,64,256]{2,1,0:T(8,128)(2,1)} %copy.111), calls=%async_computation.2 | async-start | bytes 524288 | tf_op jit(solution)/shard_map/all_to_all | solution.py:84
  100.7 11.5 %convolution_convert_fusion.4 = bf16[256,1024]{1,0:T(8,128)(2,1)S(1)} fusion(bf16[256,8192]{1,0:T(8,128)(2,1)} %all-gather.3.cloned.1.call-done, bf16[8192,1024]{1,0:T(8,128)(2,1)} %param.16), kind=kOutput, calls=%fused_computation.45 | convolution fusion | flops 4295229440 | bytes 21495808 | tf_op jit(solution)/shard_map/dot_general | solution.py:65
  116.0 4.8 collective-permute-done.9
  120.9 6.0 %all-to-all-start.1 = ((bf16[8,64,1024]{2,1,0:T(8,128)(2,1)}), bf16[8,64,1024]{2,1,0:T(8,128)(2,1)}, u32[]{:S(2)}, u32[]{:S(2)}) async-start(bf16[8,64,1024]{2,1,0:T(8,128)(2,1)} %copy.107), calls=%async_computation.1 | async-start | bytes 2097152 | tf_op jit(solution)/shard_map/all_to_all | solution.py:78
  134.7 12.6 %all-to-all-done.1 = bf16[8,64,1024]{2,1,0:T(8,128)(2,1)} async-done(((bf16[8,64,1024]{2,1,0:T(8,128)(2,1)}), bf16[8,64,1024]{2,1,0:T(8,128)(2,1)}, u32[]{:S(2)}, u32[]{:S(2)}) %all-to-all-start.1) | async-done | bytes 1048608 | tf_op jit(solution)/shard_map/all_to_all | solution.py:78
  154.7 16.3 %all-gather.5.cloned.1.call-done = bf16[2048,256]{1,0:T(8,128)(2,1)} async-done(((bf16[256,256]{1,0:T(8,128)(2,1)}), bf16[2048,256]{1,0:T(8,128)(2,1)}) %all-gather.5.cloned.1.call-update) | async-done | bytes 1048592 | tf_op jit(solution)/shard_map/all_gather | solution.py:204
  171.0 2.3 copy.116
  174.4 47.7 %while.56 = (s32[]{:T(128)}, f32[2,4,256]{2,1,0:T(4,128)S(1)}, f32[2,4,256]{2,1,0:T(4,128)S(1)}, f32[2,4,256,128]{3,2,1,0:T(8,128)}, s32[256]{0:T(256)}, /*index...) while((s32[]{:T(128)}, f32[2,4,256]{2,1,0:T(4,128)S(1)}, ...), condition=%wide.region_10.11_spmd, body=%wide.region_4.10_spmd.sunk | while | flops 1892683776 | bytes 25835900 | solution.py:220
  178.1 8.2 %conditional.5 = ((f32[2,4,256]{2,1,0:T(4,128)S(1)}, f32[2,4,256]{2,1,0:T(4,128)S(1)}, f32[2,4,256,128]{3,2,1,0:T(8,128)})) conditional(s32[]{:T(128)} %convert_element_type.201, (f32[2,4,256]{2,1,0:T(4,128)S(1)}, f32[2,4,256]{2,1,0:T(4,128)S(1)}, f32[2,4,256,128]{3,2,1,0:T(8,128)}) %tuple.116, (pred[256,512]{0,1:T(8,128)(4,1)S(1)}, ...), branch_computations={%region_6.6_spmd, %region_7.9_spmd} | conditional | flops 1892159488 | bytes 25690204 | solution.py:127
  181.1 4.2 fusion.8
  190.0 8.2 %conditional.5 = ((f32[2,4,256]{2,1,0:T(4,128)S(1)}, f32[2,4,256]{2,1,0:T(4,128)S(1)}, f32[2,4,256,128]{3,2,1,0:T(8,128)})) conditional(s32[]{:T(128)} %convert_element_type.201, (f32[2,4,256]{2,1,0:T(4,128)S(1)}, f32[2,4,256]{2,1,0:T(4,128)S(1)}, f32[2,4,256,128]{3,2,1,0:T(8,128)}) %tuple.116, (pred[256,512]{0,1:T(8,128)(4,1)S(1)}, ...), branch_computations={%region_6.6_spmd, %region_7.9_spmd} | conditional | flops 1892159488 | bytes 25690204 | solution.py:127
  193.0 4.2 fusion.8
  201.9 8.2 %conditional.5 = ((f32[2,4,256]{2,1,0:T(4,128)S(1)}, f32[2,4,256]{2,1,0:T(4,128)S(1)}, f32[2,4,256,128]{3,2,1,0:T(8,128)})) conditional(s32[]{:T(128)} %convert_element_type.201, (f32[2,4,256]{2,1,0:T(4,128)S(1)}, f32[2,4,256]{2,1,0:T(4,128)S(1)}, f32[2,4,256,128]{3,2,1,0:T(8,128)}) %tuple.116, (pred[256,512]{0,1:T(8,128)(4,1)S(1)}, ...), branch_computations={%region_6.6_spmd, %region_7.9_spmd} | conditional | flops 1892159488 | bytes 25690204 | solution.py:127
  204.9 4.2 fusion.8
  213.9 8.2 %conditional.5 = ((f32[2,4,256]{2,1,0:T(4,128)S(1)}, f32[2,4,256]{2,1,0:T(4,128)S(1)}, f32[2,4,256,128]{3,2,1,0:T(8,128)})) conditional(s32[]{:T(128)} %convert_element_type.201, (f32[2,4,256]{2,1,0:T(4,128)S(1)}, f32[2,4,256]{2,1,0:T(4,128)S(1)}, f32[2,4,256,128]{3,2,1,0:T(8,128)}) %tuple.116, (pred[256,512]{0,1:T(8,128)(4,1)S(1)}, ...), branch_computations={%region_6.6_spmd, %region_7.9_spmd} | conditional | flops 1892159488 | bytes 25690204 | solution.py:127
  216.8 4.2 fusion.8
  222.0 2.7 fusion.51
  227.0 203.8 %while.57 = (s32[]{:T(128)}, f32[256,2,4,128]{3,0,2,1:T(8,128)S(1)}, bf16[256,256]{1,0:T(8,128)(2,1)}, bf16[256,256]{1,0:T(8,128)(2,1)}, f32[256,256]{0,1:T(8,12...) while((s32[]{:T(128)}, ...), condition=%wide.region_15.16_spmd.clone, body=%wide.region_11.15_spmd.clone.sunk | while | flops 676593664 | bytes 24142468 | solution.py:241
  236.6 5.6 conditional.6
  244.9 5.5 collective-permute-done.3
  257.9 2.1 fusion.83
  260.6 5.6 conditional.6
  267.8 2.3 collective-permute-start.2
  270.4 3.6 collective-permute-done.3
  282.3 2.1 fusion.83
  285.0 5.6 conditional.6
  294.7 3.6 collective-permute-done.3
  298.4 2.4 collective-permute-done.2
  306.4 2.1 fusion.83
  309.1 5.6 %conditional.6 = (f32[256,2,4,128]{3,0,2,1:T(8,128)S(1)}, f32[256,256]{0,1:T(8,128)S(1)}, f32[256,256]{0,1:T(8,128)S(1)}) conditional(s32[]{:T(128)} %convert_element_type.204, () %tuple.120, (pred[256,256]{0,1:T(8,128)(4,1)}, bf16[256,256]{1,0:T(8,128)(2,1)}, bf16[256,2,4,128]{0,3,2,1:T(8,128)(2,1)}, f32[2,4,256]{2,1,0:T(4,128)}, ...), branch_computations={%region_13.13_spmd, %region_14.14_spmd} | conditional | flops 675282944 | bytes 16203828 | solution.py:180
  314.8 2.5 collective-permute-start.3
  319.7 2.8 collective-permute-done.3
  322.5 3.5 collective-permute-done.2
  329.9 2.6 collective-permute-start.1
  336.8 5.6 conditional.6
  344.5 6.9 %collective-permute-done.3 = bf16[256,256]{0,1:T(8,128)(2,1)S(1)} collective-permute-done((bf16[256,256]{0,1:T(8,128)(2,1)S(1)}, bf16[256,256]{0,1:T(8,128)(2,1)S(1)}, u32[]{:S(2)}, u32[]{:S(2)}) %collective-permute-start.3) | collective-permute-done | bytes 131104 | tf_op jit(solution)/shard_map/while/body/eval_jaxpr/ppermute | solution.py:16
  351.5 2.4 collective-permute-done.2
  362.0 5.6 conditional.6
  369.0 2.7 collective-permute-start.2
  372.0 4.7 collective-permute-done.3
  386.8 5.6 conditional.6
  394.5 2.4 collective-permute-start.2
  397.2 4.1 collective-permute-done.3
  406.6 2.4 collective-permute-start.1
  413.3 5.6 conditional.6
  422.0 6.1 %collective-permute-done.3 = bf16[256,256]{0,1:T(8,128)(2,1)S(1)} collective-permute-done((bf16[256,256]{0,1:T(8,128)(2,1)S(1)}, bf16[256,256]{0,1:T(8,128)(2,1)S(1)}, u32[]{:S(2)}, u32[]{:S(2)}) %collective-permute-start.3) | collective-permute-done | bytes 131104 | tf_op jit(solution)/shard_map/while/body/eval_jaxpr/ppermute | solution.py:16
  432.0 3.4 all-to-all-start.5
  437.6 6.0 %all-to-all-done.5 = bf16[8,64,256]{2,1,0:T(8,128)(2,1)S(1)} async-done(((bf16[8,64,256]{2,1,0:T(8,128)(2,1)}), bf16[8,64,256]{2,1,0:T(8,128)(2,1)S(1)}, u32[]{:S(2)}, u32[]{:S(2)}) %all-to-all-start.5) | async-done | bytes 262176 | tf_op jit(solution)/shard_map/all_to_all | solution.py:255
  443.6 3.4 all-to-all-start.4
  450.1 10.0 %all-to-all-done.4 = bf16[8,64,256]{2,1,0:T(8,128)(2,1)S(1)} async-done(((bf16[8,64,256]{2,1,0:T(8,128)(2,1)}), bf16[8,64,256]{2,1,0:T(8,128)(2,1)S(1)}, u32[]{:S(2)}, u32[]{:S(2)}) %all-to-all-start.4) | async-done | bytes 262176 | tf_op jit(solution)/shard_map/all_to_all | solution.py:252
  460.1 3.6 all-to-all-start.3
  464.3 15.6 %all-to-all-done.3 = bf16[8,64,1024]{2,1,0:T(8,128)(2,1)S(1)} async-done(((bf16[8,64,1024]{2,1,0:T(8,128)(2,1)}), bf16[8,64,1024]{2,1,0:T(8,128)(2,1)S(1)}, u32[]{:S(2)}, u32[]{:S(2)}) %all-to-all-start.3) | async-done | bytes 1048608 | tf_op jit(solution)/shard_map/all_to_all | solution.py:249
  480.9 19.2 %fusion.56 = f32[256,8192]{1,0:T(8,128)} fusion(bf16[256,1024]{1,0:T(8,128)(2,1)S(1)} %bitcast.128, bf16[8192,1024]{1,0:T(8,128)(2,1)} %param.16), kind=kOutput, calls=%fused_computation.108 | convolution fusion | flops 4294967296 | bytes 25690112 | tf_op jit(solution)/shard_map/dot_general | solution.py:44
  500.1 6.1 %convolution_add_fusion.1 = f32[256,8192]{1,0:T(8,128)S(1)} fusion(f32[256,8192]{1,0:T(8,128)} %fusion.56, bf16[256,256]{1,0:T(8,128)(2,1)S(1)} %bitcast.133, bf16[8192,256]{1,0:T(8,128)(2,1)} %param.17), kind=kOutput, calls=%fused_computation.39 | convolution fusion | flops 1075838976 | bytes 21102592 | tf_op jit(solution)/shard_map/dot_general | solution.py:44
  506.2 3.3 fusion.24
  512.1 40.4 %reduce-scatter.2.cloned.1.call-done = bf16[256,2048]{1,0:T(8,128)(2,1)} async-done(((bf16[256,8192]{1,0:T(8,128)(2,1)}), bf16[256,2048]{1,0:T(8,128)(2,1)}) %reduce-scatter.2.cloned.1.call-update) | async-done | bytes 1048592 | tf_op jit(solution)/shard_map/reduce_scatter | solution.py:274
  (359 shorter events, 204.8 us)
Async XLA Ops:
  7.2 39.6 %all-gather.3.cloned.1.call-start = ((), (), s32[]{:S(2)}) async-start(), calls=%async_computation.7 | async-start | bytes 5242880 | tf_op jit(solution)/shard_map/all_gather | solution.py:63
  8.6 105.1 %copy-start.7 = (s32[4]{0:T(128)}, s32[4]{0:T(128)S(1)}, u32[]{:S(2)}) copy-start(s32[4]{0:T(128)S(1)} %dynamic_slice.79) | copy-start | bytes 52
  8.6 49.5 %copy-start.11 = (s32[32]{0:T(128)S(1)}, s32[32]{0:T(128)}, u32[]{:S(2)}) copy-start(s32[32]{0:T(128)} %param.20) | copy-start | bytes 388
  8.6 67.7 %copy-start.12 = (s32[8]{0:T(128)S(1)}, s32[8]{0:T(128)}, u32[]{:S(2)}) copy-start(s32[8]{0:T(128)} %param.19) | copy-start | bytes 100
  8.6 72.5 %copy-start.6 = (bf16[256,1024]{1,0:T(8,128)(2,1)S(1)}, bf16[256,1024]{1,0:T(8,128)(2,1)}, u32[]{:S(2)}) copy-start(bf16[256,1024]{1,0:T(8,128)(2,1)} %param.21) | copy-start | bytes 1572868
  52.6 14.8 %all-to-all-start = ((bf16[8,64,256]{2,1,0:T(8,128)(2,1)}), bf16[8,64,256]{2,1,0:T(8,128)(2,1)S(1)}, u32[]{:S(2)}, u32[]{:S(2)}) async-start(bf16[8,64,256]{2,1,0:T(8,128)(2,1)} %copy.103), calls=%async_computation | async-start | bytes 524288 | tf_op jit(solution)/shard_map/all_to_all | solution.py:81
  58.5 88.8 %copy-start.9 = (s32[4]{0:T(128)}, s32[4]{0:T(128)S(1)}, u32[]{:S(2)}) copy-start(s32[4]{0:T(128)S(1)} %and_select_fusion) | copy-start | bytes 52
  68.4 7.9 %collective-permute-start.4 = (bf16[256,256]{1,0:T(8,128)(2,1)}, bf16[256,256]{1,0:T(8,128)(2,1)S(1)}, u32[]{:S(2)}, u32[]{:S(2)}) collective-permute-start(bf16[256,256]{1,0:T(8,128)(2,1)} %bitcast.26), channel_id=1, source_target_pairs={{0,4},{4,8},{8,12},{12,16},{16,20},{20,24},{24,28},{28,0},{1,5},{5... | collective-permute-start | bytes 393224 | tf_op jit(solution)/shard_map/ppermute | solution.py:196
  76.3 7.7 %collective-permute-start.5 = (bf16[256,256]{1,0:T(8,128)(2,1)S(1)}, bf16[256,256]{1,0:T(8,128)(2,1)S(1)}, u32[]{:S(2)}, u32[]{:S(2)}) collective-permute-start(bf16[256,256]{1,0:T(8,128)(2,1)S(1)} %collective-permute-done.4), channel_id=1, source_target_pairs={{0,4},{4,8},{8,12},{12,16},{16,20},{20,24},{24,28},{28,0},{1,5},{5... | collective-permute-start | bytes 393224 | tf_op jit(solution)/shard_map/ppermute | solution.py:196
  83.9 7.7 %collective-permute-start.6 = (bf16[256,256]{1,0:T(8,128)(2,1)S(1)}, bf16[256,256]{1,0:T(8,128)(2,1)S(1)}, u32[]{:S(2)}, u32[]{:S(2)}) collective-permute-start(bf16[256,256]{1,0:T(8,128)(2,1)S(1)} %collective-permute-done.5), channel_id=1, source_target_pairs={{0,4},{4,8},{8,12},{12,16},{16,20},{20,24},{24,28},{28,0},{1,5},{5... | collective-permute-start | bytes 393224 | tf_op jit(solution)/shard_map/ppermute | solution.py:196
  91.6 8.4 %collective-permute-start.7 = (bf16[256,256]{1,0:T(8,128)(2,1)S(1)}, bf16[256,256]{1,0:T(8,128)(2,1)S(1)}, u32[]{:S(2)}, u32[]{:S(2)}) collective-permute-start(bf16[256,256]{1,0:T(8,128)(2,1)S(1)} %collective-permute-done.6), channel_id=1, source_target_pairs={{0,4},{4,8},{8,12},{12,16},{16,20},{20,24},{24,28},{28,0},{1,5},{5... | collective-permute-start | bytes 393224 | tf_op jit(solution)/shard_map/ppermute | solution.py:196
  92.7 28.2 %all-to-all-start.2 = ((bf16[8,64,256]{2,1,0:T(8,128)(2,1)}), bf16[8,64,256]{2,1,0:T(8,128)(2,1)S(1)}, u32[]{:S(2)}, u32[]{:S(2)}) async-start(bf16[8,64,256]{2,1,0:T(8,128)(2,1)} %copy.111), calls=%async_computation.2 | async-start | bytes 524288 | tf_op jit(solution)/shard_map/all_to_all | solution.py:84
  100.0 12.3 %collective-permute-start.8 = (bf16[256,256]{1,0:T(8,128)(2,1)S(1)}, bf16[256,256]{1,0:T(8,128)(2,1)S(1)}, u32[]{:S(2)}, u32[]{:S(2)}) collective-permute-start(bf16[256,256]{1,0:T(8,128)(2,1)S(1)} %collective-permute-done.7), channel_id=1, source_target_pairs={{0,4},{4,8},{8,12},{12,16},{16,20},{20,24},{24,28},{28,0},{1,5},{5... | collective-permute-start | bytes 393224 | tf_op jit(solution)/shard_map/ppermute | solution.py:196
  112.3 8.6 %collective-permute-start.9 = (bf16[256,256]{1,0:T(8,128)(2,1)S(1)}, bf16[256,256]{1,0:T(8,128)(2,1)S(1)}, u32[]{:S(2)}, u32[]{:S(2)}) collective-permute-start(bf16[256,256]{1,0:T(8,128)(2,1)S(1)} %collective-permute-done.8), channel_id=1, source_target_pairs={{0,4},{4,8},{8,12},{12,16},{16,20},{20,24},{24,28},{28,0},{1,5},{5... | collective-permute-start | bytes 393224 | tf_op jit(solution)/shard_map/ppermute | solution.py:196
  120.9 9.2 %collective-permute-start.10 = (bf16[256,256]{1,0:T(8,128)(2,1)S(1)}, bf16[256,256]{1,0:T(8,128)(2,1)S(1)}, u32[]{:S(2)}, u32[]{:S(2)}) collective-permute-start(bf16[256,256]{1,0:T(8,128)(2,1)S(1)} %collective-permute-done.9), channel_id=1, source_target_pairs={{0,4},{4,8},{8,12},{12,16},{16,20},{20,24},{24,28},{28,0},{1,5},{5... | collective-permute-start | bytes 393224 | tf_op jit(solution)/shard_map/ppermute | solution.py:196
  120.9 26.4 %all-to-all-start.1 = ((bf16[8,64,1024]{2,1,0:T(8,128)(2,1)}), bf16[8,64,1024]{2,1,0:T(8,128)(2,1)}, u32[]{:S(2)}, u32[]{:S(2)}) async-start(bf16[8,64,1024]{2,1,0:T(8,128)(2,1)} %copy.107), calls=%async_computation.1 | async-start | bytes 2097152 | tf_op jit(solution)/shard_map/all_to_all | solution.py:78
  126.9 44.2 %all-gather.5.cloned.1.call-start = ((), (), s32[]{:S(2)}) async-start(), calls=%async_computation.8 | async-start | bytes 1179648 | tf_op jit(solution)/shard_map/all_gather | solution.py:204
  227.0 203.9 %copy-start.10 = (s32[4]{0:T(128)S(1)}, s32[4]{0:T(128)}, u32[]{:S(2)}) copy-start(s32[4]{0:T(128)} %copy-done.9) | copy-start | bytes 52
  228.8 23.7 %collective-permute-start = (bf16[256,256]{1,0:T(8,128)(2,1)}, bf16[256,256]{1,0:T(8,128)(2,1)}, u32[]{:S(2)}, u32[]{:S(2)}) collective-permute-start(bf16[256,256]{1,0:T(8,128)(2,1)} %copy.242), channel_id=1, source_target_pairs={{0,4},{4,8},{8,12},{12,16},{16,20},{20,24},{24,28},{28,0},{1,5},{5... | collective-permute-start | bytes 393224 | tf_op jit(solution)/shard_map/while/body/eval_jaxpr/ppermute | solution.py:16
  231.0 21.6 %collective-permute-start.1 = (bf16[256,256]{1,0:T(8,128)(2,1)}, bf16[256,256]{1,0:T(8,128)(2,1)}, u32[]{:S(2)}, u32[]{:S(2)}) collective-permute-start(bf16[256,256]{1,0:T(8,128)(2,1)} %copy.243), channel_id=1, source_target_pairs={{0,4},{4,8},{8,12},{12,16},{16,20},{20,24},{24,28},{28,0},{1,5},{5... | collective-permute-start | bytes 393224 | tf_op jit(solution)/shard_map/while/body/eval_jaxpr/ppermute | solution.py:16
  238.5 2.6 copy-start
  242.3 8.2 %collective-permute-start.3 = (bf16[256,256]{0,1:T(8,128)(2,1)S(1)}, bf16[256,256]{0,1:T(8,128)(2,1)S(1)}, u32[]{:S(2)}, u32[]{:S(2)}) collective-permute-start(bf16[256,256]{0,1:T(8,128)(2,1)S(1)} %fusion.85), channel_id=1, source_target_pairs={{0,4},{4,8},{8,12},{12,16},{16,20},{20,24},{24,28},{28,0},{1,5},{5... | collective-permute-start | bytes 393224 | tf_op jit(solution)/shard_map/while/body/eval_jaxpr/ppermute | solution.py:16
  242.9 8.9 %collective-permute-start.2 = (bf16[256,256]{0,1:T(8,128)(2,1)S(1)}, bf16[256,256]{0,1:T(8,128)(2,1)S(1)}, u32[]{:S(2)}, u32[]{:S(2)}) collective-permute-start(bf16[256,256]{0,1:T(8,128)(2,1)S(1)} %fusion.84), channel_id=1, source_target_pairs={{0,4},{4,8},{8,12},{12,16},{16,20},{20,24},{24,28},{28,0},{1,5},{5... | collective-permute-start | bytes 393224 | tf_op jit(solution)/shard_map/while/body/eval_jaxpr/ppermute | solution.py:16
  254.1 22.1 %collective-permute-start = (bf16[256,256]{1,0:T(8,128)(2,1)}, bf16[256,256]{1,0:T(8,128)(2,1)}, u32[]{:S(2)}, u32[]{:S(2)}) collective-permute-start(bf16[256,256]{1,0:T(8,128)(2,1)} %copy.242), channel_id=1, source_target_pairs={{0,4},{4,8},{8,12},{12,16},{16,20},{20,24},{24,28},{28,0},{1,5},{5... | collective-permute-start | bytes 393224 | tf_op jit(solution)/shard_map/while/body/eval_jaxpr/ppermute | solution.py:16
  255.7 20.5 %collective-permute-start.1 = (bf16[256,256]{1,0:T(8,128)(2,1)}, bf16[256,256]{1,0:T(8,128)(2,1)}, u32[]{:S(2)}, u32[]{:S(2)}) collective-permute-start(bf16[256,256]{1,0:T(8,128)(2,1)} %copy.243), channel_id=1, source_target_pairs={{0,4},{4,8},{8,12},{12,16},{16,20},{20,24},{24,28},{28,0},{1,5},{5... | collective-permute-start | bytes 393224 | tf_op jit(solution)/shard_map/while/body/eval_jaxpr/ppermute | solution.py:16
  262.5 2.6 copy-start
  266.2 7.7 %collective-permute-start.3 = (bf16[256,256]{0,1:T(8,128)(2,1)S(1)}, bf16[256,256]{0,1:T(8,128)(2,1)S(1)}, u32[]{:S(2)}, u32[]{:S(2)}) collective-permute-start(bf16[256,256]{0,1:T(8,128)(2,1)S(1)} %fusion.85), channel_id=1, source_target_pairs={{0,4},{4,8},{8,12},{12,16},{16,20},{20,24},{24,28},{28,0},{1,5},{5... | collective-permute-start | bytes 393224 | tf_op jit(solution)/shard_map/while/body/eval_jaxpr/ppermute | solution.py:16
  267.8 7.7 %collective-permute-start.2 = (bf16[256,256]{0,1:T(8,128)(2,1)S(1)}, bf16[256,256]{0,1:T(8,128)(2,1)S(1)}, u32[]{:S(2)}, u32[]{:S(2)}) collective-permute-start(bf16[256,256]{0,1:T(8,128)(2,1)S(1)} %fusion.84), channel_id=1, source_target_pairs={{0,4},{4,8},{8,12},{12,16},{16,20},{20,24},{24,28},{28,0},{1,5},{5... | collective-permute-start | bytes 393224 | tf_op jit(solution)/shard_map/while/body/eval_jaxpr/ppermute | solution.py:16
  277.8 23.8 %collective-permute-start = (bf16[256,256]{1,0:T(8,128)(2,1)}, bf16[256,256]{1,0:T(8,128)(2,1)}, u32[]{:S(2)}, u32[]{:S(2)}) collective-permute-start(bf16[256,256]{1,0:T(8,128)(2,1)} %copy.242), channel_id=1, source_target_pairs={{0,4},{4,8},{8,12},{12,16},{16,20},{20,24},{24,28},{28,0},{1,5},{5... | collective-permute-start | bytes 393224 | tf_op jit(solution)/shard_map/while/body/eval_jaxpr/ppermute | solution.py:16
  279.4 22.2 %collective-permute-start.1 = (bf16[256,256]{1,0:T(8,128)(2,1)}, bf16[256,256]{1,0:T(8,128)(2,1)}, u32[]{:S(2)}, u32[]{:S(2)}) collective-permute-start(bf16[256,256]{1,0:T(8,128)(2,1)} %copy.243), channel_id=1, source_target_pairs={{0,4},{4,8},{8,12},{12,16},{16,20},{20,24},{24,28},{28,0},{1,5},{5... | collective-permute-start | bytes 393224 | tf_op jit(solution)/shard_map/while/body/eval_jaxpr/ppermute | solution.py:16
  286.9 2.6 copy-start
  290.7 7.7 %collective-permute-start.3 = (bf16[256,256]{0,1:T(8,128)(2,1)S(1)}, bf16[256,256]{0,1:T(8,128)(2,1)S(1)}, u32[]{:S(2)}, u32[]{:S(2)}) collective-permute-start(bf16[256,256]{0,1:T(8,128)(2,1)S(1)} %fusion.85), channel_id=1, source_target_pairs={{0,4},{4,8},{8,12},{12,16},{16,20},{20,24},{24,28},{28,0},{1,5},{5... | collective-permute-start | bytes 393224 | tf_op jit(solution)/shard_map/while/body/eval_jaxpr/ppermute | solution.py:16
  293.1 7.7 %collective-permute-start.2 = (bf16[256,256]{0,1:T(8,128)(2,1)S(1)}, bf16[256,256]{0,1:T(8,128)(2,1)S(1)}, u32[]{:S(2)}, u32[]{:S(2)}) collective-permute-start(bf16[256,256]{0,1:T(8,128)(2,1)S(1)} %fusion.84), channel_id=1, source_target_pairs={{0,4},{4,8},{8,12},{12,16},{16,20},{20,24},{24,28},{28,0},{1,5},{5... | collective-permute-start | bytes 393224 | tf_op jit(solution)/shard_map/while/body/eval_jaxpr/ppermute | solution.py:16
  303.1 23.7 %collective-permute-start = (bf16[256,256]{1,0:T(8,128)(2,1)}, bf16[256,256]{1,0:T(8,128)(2,1)}, u32[]{:S(2)}, u32[]{:S(2)}) collective-permute-start(bf16[256,256]{1,0:T(8,128)(2,1)} %copy.242), channel_id=1, source_target_pairs={{0,4},{4,8},{8,12},{12,16},{16,20},{20,24},{24,28},{28,0},{1,5},{5... | collective-permute-start | bytes 393224 | tf_op jit(solution)/shard_map/while/body/eval_jaxpr/ppermute | solution.py:16
  304.7 22.1 %collective-permute-start.1 = (bf16[256,256]{1,0:T(8,128)(2,1)}, bf16[256,256]{1,0:T(8,128)(2,1)}, u32[]{:S(2)}, u32[]{:S(2)}) collective-permute-start(bf16[256,256]{1,0:T(8,128)(2,1)} %copy.243), channel_id=1, source_target_pairs={{0,4},{4,8},{8,12},{12,16},{16,20},{20,24},{24,28},{28,0},{1,5},{5... | collective-permute-start | bytes 393224 | tf_op jit(solution)/shard_map/while/body/eval_jaxpr/ppermute | solution.py:16
  311.0 2.6 copy-start
  314.8 7.7 %collective-permute-start.3 = (bf16[256,256]{0,1:T(8,128)(2,1)S(1)}, bf16[256,256]{0,1:T(8,128)(2,1)S(1)}, u32[]{:S(2)}, u32[]{:S(2)}) collective-permute-start(bf16[256,256]{0,1:T(8,128)(2,1)S(1)} %fusion.85), channel_id=1, source_target_pairs={{0,4},{4,8},{8,12},{12,16},{16,20},{20,24},{24,28},{28,0},{1,5},{5... | collective-permute-start | bytes 393224 | tf_op jit(solution)/shard_map/while/body/eval_jaxpr/ppermute | solution.py:16
  318.3 7.8 %collective-permute-start.2 = (bf16[256,256]{0,1:T(8,128)(2,1)S(1)}, bf16[256,256]{0,1:T(8,128)(2,1)S(1)}, u32[]{:S(2)}, u32[]{:S(2)}) collective-permute-start(bf16[256,256]{0,1:T(8,128)(2,1)S(1)} %fusion.84), channel_id=1, source_target_pairs={{0,4},{4,8},{8,12},{12,16},{16,20},{20,24},{24,28},{28,0},{1,5},{5... | collective-permute-start | bytes 393224 | tf_op jit(solution)/shard_map/while/body/eval_jaxpr/ppermute | solution.py:16
  328.4 26.2 %collective-permute-start = (bf16[256,256]{1,0:T(8,128)(2,1)}, bf16[256,256]{1,0:T(8,128)(2,1)}, u32[]{:S(2)}, u32[]{:S(2)}) collective-permute-start(bf16[256,256]{1,0:T(8,128)(2,1)} %copy.242), channel_id=1, source_target_pairs={{0,4},{4,8},{8,12},{12,16},{16,20},{20,24},{24,28},{28,0},{1,5},{5... | collective-permute-start | bytes 393224 | tf_op jit(solution)/shard_map/while/body/eval_jaxpr/ppermute | solution.py:16
  329.9 24.7 %collective-permute-start.1 = (bf16[256,256]{1,0:T(8,128)(2,1)}, bf16[256,256]{1,0:T(8,128)(2,1)}, u32[]{:S(2)}, u32[]{:S(2)}) collective-permute-start(bf16[256,256]{1,0:T(8,128)(2,1)} %copy.243), channel_id=1, source_target_pairs={{0,4},{4,8},{8,12},{12,16},{16,20},{20,24},{24,28},{28,0},{1,5},{5... | collective-permute-start | bytes 393224 | tf_op jit(solution)/shard_map/while/body/eval_jaxpr/ppermute | solution.py:16
  338.7 2.6 copy-start
  342.4 9.0 %collective-permute-start.3 = (bf16[256,256]{0,1:T(8,128)(2,1)S(1)}, bf16[256,256]{0,1:T(8,128)(2,1)S(1)}, u32[]{:S(2)}, u32[]{:S(2)}) collective-permute-start(bf16[256,256]{0,1:T(8,128)(2,1)S(1)} %fusion.85), channel_id=1, source_target_pairs={{0,4},{4,8},{8,12},{12,16},{16,20},{20,24},{24,28},{28,0},{1,5},{5... | collective-permute-start | bytes 393224 | tf_op jit(solution)/shard_map/while/body/eval_jaxpr/ppermute | solution.py:16
  344.1 9.8 %collective-permute-start.2 = (bf16[256,256]{0,1:T(8,128)(2,1)S(1)}, bf16[256,256]{0,1:T(8,128)(2,1)S(1)}, u32[]{:S(2)}, u32[]{:S(2)}) collective-permute-start(bf16[256,256]{0,1:T(8,128)(2,1)S(1)} %fusion.84), channel_id=1, source_target_pairs={{0,4},{4,8},{8,12},{12,16},{16,20},{20,24},{24,28},{28,0},{1,5},{5... | collective-permute-start | bytes 393224 | tf_op jit(solution)/shard_map/while/body/eval_jaxpr/ppermute | solution.py:16
  356.2 22.7 %collective-permute-start = (bf16[256,256]{1,0:T(8,128)(2,1)}, bf16[256,256]{1,0:T(8,128)(2,1)}, u32[]{:S(2)}, u32[]{:S(2)}) collective-permute-start(bf16[256,256]{1,0:T(8,128)(2,1)} %copy.242), channel_id=1, source_target_pairs={{0,4},{4,8},{8,12},{12,16},{16,20},{20,24},{24,28},{28,0},{1,5},{5... | collective-permute-start | bytes 393224 | tf_op jit(solution)/shard_map/while/body/eval_jaxpr/ppermute | solution.py:16
  357.7 21.1 %collective-permute-start.1 = (bf16[256,256]{1,0:T(8,128)(2,1)}, bf16[256,256]{1,0:T(8,128)(2,1)}, u32[]{:S(2)}, u32[]{:S(2)}) collective-permute-start(bf16[256,256]{1,0:T(8,128)(2,1)} %copy.243), channel_id=1, source_target_pairs={{0,4},{4,8},{8,12},{12,16},{16,20},{20,24},{24,28},{28,0},{1,5},{5... | collective-permute-start | bytes 393224 | tf_op jit(solution)/shard_map/while/body/eval_jaxpr/ppermute | solution.py:16
  363.9 2.6 copy-start
  367.6 9.1 %collective-permute-start.3 = (bf16[256,256]{0,1:T(8,128)(2,1)S(1)}, bf16[256,256]{0,1:T(8,128)(2,1)S(1)}, u32[]{:S(2)}, u32[]{:S(2)}) collective-permute-start(bf16[256,256]{0,1:T(8,128)(2,1)S(1)} %fusion.85), channel_id=1, source_target_pairs={{0,4},{4,8},{8,12},{12,16},{16,20},{20,24},{24,28},{28,0},{1,5},{5... | collective-permute-start | bytes 393224 | tf_op jit(solution)/shard_map/while/body/eval_jaxpr/ppermute | solution.py:16
  369.0 9.1 %collective-permute-start.2 = (bf16[256,256]{0,1:T(8,128)(2,1)S(1)}, bf16[256,256]{0,1:T(8,128)(2,1)S(1)}, u32[]{:S(2)}, u32[]{:S(2)}) collective-permute-start(bf16[256,256]{0,1:T(8,128)(2,1)S(1)} %fusion.84), channel_id=1, source_target_pairs={{0,4},{4,8},{8,12},{12,16},{16,20},{20,24},{24,28},{28,0},{1,5},{5... | collective-permute-start | bytes 393224 | tf_op jit(solution)/shard_map/while/body/eval_jaxpr/ppermute | solution.py:16
  380.4 23.0 %collective-permute-start = (bf16[256,256]{1,0:T(8,128)(2,1)}, bf16[256,256]{1,0:T(8,128)(2,1)}, u32[]{:S(2)}, u32[]{:S(2)}) collective-permute-start(bf16[256,256]{1,0:T(8,128)(2,1)} %copy.242), channel_id=1, source_target_pairs={{0,4},{4,8},{8,12},{12,16},{16,20},{20,24},{24,28},{28,0},{1,5},{5... | collective-permute-start | bytes 393224 | tf_op jit(solution)/shard_map/while/body/eval_jaxpr/ppermute | solution.py:16
  382.0 21.5 %collective-permute-start.1 = (bf16[256,256]{1,0:T(8,128)(2,1)}, bf16[256,256]{1,0:T(8,128)(2,1)}, u32[]{:S(2)}, u32[]{:S(2)}) collective-permute-start(bf16[256,256]{1,0:T(8,128)(2,1)} %copy.243), channel_id=1, source_target_pairs={{0,4},{4,8},{8,12},{12,16},{16,20},{20,24},{24,28},{28,0},{1,5},{5... | collective-permute-start | bytes 393224 | tf_op jit(solution)/shard_map/while/body/eval_jaxpr/ppermute | solution.py:16
  388.7 2.6 copy-start
  392.4 8.9 %collective-permute-start.3 = (bf16[256,256]{0,1:T(8,128)(2,1)S(1)}, bf16[256,256]{0,1:T(8,128)(2,1)S(1)}, u32[]{:S(2)}, u32[]{:S(2)}) collective-permute-start(bf16[256,256]{0,1:T(8,128)(2,1)S(1)} %fusion.85), channel_id=1, source_target_pairs={{0,4},{4,8},{8,12},{12,16},{16,20},{20,24},{24,28},{28,0},{1,5},{5... | collective-permute-start | bytes 393224 | tf_op jit(solution)/shard_map/while/body/eval_jaxpr/ppermute | solution.py:16
  394.5 8.3 %collective-permute-start.2 = (bf16[256,256]{0,1:T(8,128)(2,1)S(1)}, bf16[256,256]{0,1:T(8,128)(2,1)S(1)}, u32[]{:S(2)}, u32[]{:S(2)}) collective-permute-start(bf16[256,256]{0,1:T(8,128)(2,1)S(1)} %fusion.84), channel_id=1, source_target_pairs={{0,4},{4,8},{8,12},{12,16},{16,20},{20,24},{24,28},{28,0},{1,5},{5... | collective-permute-start | bytes 393224 | tf_op jit(solution)/shard_map/while/body/eval_jaxpr/ppermute | solution.py:16
  405.0 25.8 %collective-permute-start = (bf16[256,256]{1,0:T(8,128)(2,1)}, bf16[256,256]{1,0:T(8,128)(2,1)}, u32[]{:S(2)}, u32[]{:S(2)}) collective-permute-start(bf16[256,256]{1,0:T(8,128)(2,1)} %copy.242), channel_id=1, source_target_pairs={{0,4},{4,8},{8,12},{12,16},{16,20},{20,24},{24,28},{28,0},{1,5},{5... | collective-permute-start | bytes 393224 | tf_op jit(solution)/shard_map/while/body/eval_jaxpr/ppermute | solution.py:16
  406.6 24.2 %collective-permute-start.1 = (bf16[256,256]{1,0:T(8,128)(2,1)}, bf16[256,256]{1,0:T(8,128)(2,1)}, u32[]{:S(2)}, u32[]{:S(2)}) collective-permute-start(bf16[256,256]{1,0:T(8,128)(2,1)} %copy.243), channel_id=1, source_target_pairs={{0,4},{4,8},{8,12},{12,16},{16,20},{20,24},{24,28},{28,0},{1,5},{5... | collective-permute-start | bytes 393224 | tf_op jit(solution)/shard_map/while/body/eval_jaxpr/ppermute | solution.py:16
  415.2 2.6 copy-start
  418.9 9.1 %collective-permute-start.3 = (bf16[256,256]{0,1:T(8,128)(2,1)S(1)}, bf16[256,256]{0,1:T(8,128)(2,1)S(1)}, u32[]{:S(2)}, u32[]{:S(2)}) collective-permute-start(bf16[256,256]{0,1:T(8,128)(2,1)S(1)} %fusion.85), channel_id=1, source_target_pairs={{0,4},{4,8},{8,12},{12,16},{16,20},{20,24},{24,28},{28,0},{1,5},{5... | collective-permute-start | bytes 393224 | tf_op jit(solution)/shard_map/while/body/eval_jaxpr/ppermute | solution.py:16
  420.3 9.8 %collective-permute-start.2 = (bf16[256,256]{0,1:T(8,128)(2,1)S(1)}, bf16[256,256]{0,1:T(8,128)(2,1)S(1)}, u32[]{:S(2)}, u32[]{:S(2)}) collective-permute-start(bf16[256,256]{0,1:T(8,128)(2,1)S(1)} %fusion.84), channel_id=1, source_target_pairs={{0,4},{4,8},{8,12},{12,16},{16,20},{20,24},{24,28},{28,0},{1,5},{5... | collective-permute-start | bytes 393224 | tf_op jit(solution)/shard_map/while/body/eval_jaxpr/ppermute | solution.py:16
  432.0 11.6 %all-to-all-start.5 = ((bf16[8,64,256]{2,1,0:T(8,128)(2,1)}), bf16[8,64,256]{2,1,0:T(8,128)(2,1)S(1)}, u32[]{:S(2)}, u32[]{:S(2)}) async-start(bf16[8,64,256]{2,1,0:T(8,128)(2,1)} %copy.132), calls=%async_computation.5 | async-start | bytes 524288 | tf_op jit(solution)/shard_map/all_to_all | solution.py:255
  443.6 16.5 %all-to-all-start.4 = ((bf16[8,64,256]{2,1,0:T(8,128)(2,1)}), bf16[8,64,256]{2,1,0:T(8,128)(2,1)S(1)}, u32[]{:S(2)}, u32[]{:S(2)}) async-start(bf16[8,64,256]{2,1,0:T(8,128)(2,1)} %copy.127), calls=%async_computation.4 | async-start | bytes 524288 | tf_op jit(solution)/shard_map/all_to_all | solution.py:252
  447.1 16.6 %copy-start.8 = (s32[4]{0:T(128)S(1)}, s32[4]{0:T(128)}, u32[]{:S(2)}) copy-start(s32[4]{0:T(128)} %copy-done.7) | copy-start | bytes 52
  460.1 19.9 %all-to-all-start.3 = ((bf16[8,64,1024]{2,1,0:T(8,128)(2,1)}), bf16[8,64,1024]{2,1,0:T(8,128)(2,1)S(1)}, u32[]{:S(2)}, u32[]{:S(2)}) async-start(bf16[8,64,1024]{2,1,0:T(8,128)(2,1)} %copy.122), calls=%async_computation.3 | async-start | bytes 2097152 | tf_op jit(solution)/shard_map/all_to_all | solution.py:249
  463.6 88.9 %reduce-scatter.2.cloned.1.call-start = ((), (), s32[]{:S(2)}) async-start(), calls=%async_computation.9 | async-start | bytes 5242880 | tf_op jit(solution)/shard_map/reduce_scatter | solution.py:274
  500.1 6.1 %copy-start.4 = (bf16[8192,256]{1,0:T(8,128)(2,1)S(1)}, bf16[8192,256]{1,0:T(8,128)(2,1)}, u32[]{:S(2)}) copy-start(bf16[8192,256]{1,0:T(8,128)(2,1)} %param.18) | copy-start | bytes 12582916
  (10 other events, 13.6 us)
Sparse Core Ops, SparseCore 0:
  9.6 37.1 all-gather.2
  129.8 41.1 all-gather.4
  509.6 42.8 reduce-scatter.1
